TPU v7x, 32 devices: a whole 2x2x4 slice. The times are simulated.
32 devices in a mesh: layer: 4 (over y, x), strip: 8 (over z, core).
Axes of the slice: x: 2, y: 2, z: 4, core: 2. Of those that a mesh axis runs over, the one named last changes fastest.
Arguments:
- launch: bfloat16 [2, 2, 1024, 1024], P(None, None, 'strip'), may hold values from -6 to 6
- screens: float32 [4, 1024, 1024], P('layer', 'strip'), may hold values from -3.140625 to 3.140625
- distance: float32 [4], P('layer'), may hold values from 1024 to 2048
- templates: bfloat16 [1024, 16], replicated, may hold values from -0.1875 to 0.1875
- send_table: int32 [8, 8, 4], P('strip', None, 'layer'), may hold values from 0 to 511, as said below
- send_counts: int32 [8, 8], P('strip'), may hold values from 0 to 4, as said below
Outputs:
- pupil: bfloat16 [2, 2, 1024, 1024], P(None, None, 'strip')
- correlation: float32 [8, 8, 4, 2, 16], P('strip', None, 'layer')
Inputs may be any that keep to these rules, and one draw needn't show every extreme that they name: For each source strip s the 8 x 4 entries send_table[s] are distinct subaperture numbers local to that strip (row by row over its 512 subapertures). `send_counts`: some owner receives 4 live slots from every source.
All inputs are finite; a program needn't handle non-finite values.
Results may differ from a plain program's by a relative error of at most 0.03.
Values may be sent and summed in bfloat16 or wider, within the bound.
A program may use at most 64 MiB of HBM per device.

v0:
```python
import math

import jax
import jax.numpy as jnp
from jax import lax
from jax.sharding import PartitionSpec as P

SUB = 16


def passed_along(value, axis, steps):
    count = lax.axis_size(axis)
    first, last = (max(0, -steps), min(count, count - steps))
    return lax.ppermute(value, axis, [(source, source + steps) for source in range(first, last)])


def broadcast(x, axis, root):
    mine = lax.axis_index(axis) == root
    return lax.psum(jnp.where(mine, x, jnp.zeros_like(x)), axis)


def fourier_tables(length):
    counter = jnp.arange(length, dtype=jnp.int32)
    product = counter[:, None] * counter[None, :] % length
    angles = product.astype(jnp.float32) * (2.0 * math.pi / length)
    factor = 1.0 / math.sqrt(length)
    return (
        (jnp.cos(angles) * factor).astype(jnp.bfloat16),
        (jnp.sin(angles) * factor).astype(jnp.bfloat16),
    )


def spectral_factor(distance_value, length):
    counter = jnp.arange(length, dtype=jnp.int32)
    signed = jnp.where(counter < length // 2, counter, counter - length).astype(jnp.float32)
    phases = -distance_value * math.pi * signed * signed / float(length * length)
    return (jnp.cos(phases), jnp.sin(phases))


def spot_table(subsize):
    spotsize = 2 * subsize
    outer = jnp.arange(spotsize, dtype=jnp.int32)
    inner = jnp.arange(subsize, dtype=jnp.int32)
    angles = (inner[:, None] * outer[None, :] % spotsize).astype(jnp.float32) * (
        2.0 * math.pi / spotsize
    )
    wave_re = jnp.cos(angles) / math.sqrt(subsize)
    wave_im = -jnp.sin(angles) / math.sqrt(subsize)
    kron_re = (
        wave_re[:, None, :, None] * wave_re[None, :, None, :]
        - wave_im[:, None, :, None] * wave_im[None, :, None, :]
    )
    kron_im = (
        wave_re[:, None, :, None] * wave_im[None, :, None, :]
        + wave_im[:, None, :, None] * wave_re[None, :, None, :]
    )
    kron_re = kron_re.reshape(subsize * subsize, spotsize * spotsize)
    kron_im = kron_im.reshape(subsize * subsize, spotsize * spotsize)
    upper = jnp.concatenate([kron_re, kron_im], axis=1)
    lower = jnp.concatenate([-kron_im, kron_re], axis=1)
    return jnp.concatenate([upper, lower], axis=0).astype(jnp.bfloat16)


def correlate_slots(slots, big_table, templates):
    pixels = templates.shape[0]
    fields_count = slots.shape[-1] // big_table.shape[0]
    shaped = slots.reshape(slots.shape[:-1] + (fields_count, big_table.shape[0]))
    spot_field = jnp.einsum("...i,io->...o", shaped, big_table, preferred_element_type=jnp.float32)
    intensity = (
        spot_field[..., :pixels] * spot_field[..., :pixels]
        + spot_field[..., pixels:] * spot_field[..., pixels:]
    )
    intensity = intensity.astype(jnp.bfloat16)
    return jnp.einsum("...i,io->...o", intensity, templates, preferred_element_type=jnp.float32)


def layer_step(field, screen, distance_value, cosine_table, sine_table, pieces):
    strip_rows = field.shape[1]
    length = field.shape[2]
    real_part = field[0].astype(jnp.float32)
    imag_part = field[1].astype(jnp.float32)
    screen_cos = jnp.cos(screen)
    screen_sin = jnp.sin(screen)
    screened = jnp.stack(
        [
            real_part * screen_cos - imag_part * screen_sin,
            real_part * screen_sin + imag_part * screen_cos,
        ]
    ).astype(jnp.bfloat16)
    factor_re, factor_im = spectral_factor(distance_value, length)
    along_cos = jnp.einsum(
        "prj,jk->kpr", screened, cosine_table, preferred_element_type=jnp.float32
    )
    along_sin = jnp.einsum("prj,jk->kpr", screened, sine_table, preferred_element_type=jnp.float32)
    freq_re = along_cos[:, 0] + along_sin[:, 1]
    freq_im = along_cos[:, 1] - along_sin[:, 0]
    column_re = factor_re[:, None]
    column_im = factor_im[:, None]
    spectrum = jnp.stack(
        [freq_re * column_re - freq_im * column_im, freq_re * column_im + freq_im * column_re],
        axis=1,
    ).astype(jnp.bfloat16)
    spectrum = spectrum.reshape(pieces, length // pieces, 2, strip_rows)
    columns = lax.all_to_all(spectrum, "strip", split_axis=0, concat_axis=3, tiled=True)
    row_cos = jnp.einsum("acpj,jk->acpk", columns, cosine_table, preferred_element_type=jnp.float32)
    row_sin = jnp.einsum("acpj,jk->acpk", columns, sine_table, preferred_element_type=jnp.float32)
    wave_re = row_cos[:, :, 0] + row_sin[:, :, 1]
    wave_im = row_cos[:, :, 1] - row_sin[:, :, 0]
    phased = jnp.stack(
        [wave_re * factor_re - wave_im * factor_im, wave_re * factor_im + wave_im * factor_re],
        axis=2,
    ).astype(jnp.bfloat16)
    back_cos = jnp.einsum("acpj,kj->acpk", phased, cosine_table, preferred_element_type=jnp.float32)
    back_sin = jnp.einsum("acpj,kj->acpk", phased, sine_table, preferred_element_type=jnp.float32)
    columns_done = jnp.stack(
        [back_cos[:, :, 0] - back_sin[:, :, 1], back_cos[:, :, 1] + back_sin[:, :, 0]], axis=2
    ).astype(jnp.bfloat16)
    column_count = columns_done.shape[1]
    regrouped = columns_done.reshape(column_count, 2, pieces, strip_rows)
    returned = lax.all_to_all(regrouped, "strip", split_axis=2, concat_axis=0, tiled=True)
    returned = returned.reshape(length, 2, strip_rows)
    final_cos = jnp.einsum(
        "kpr,kj->prj", returned, cosine_table, preferred_element_type=jnp.float32
    )
    final_sin = jnp.einsum("kpr,kj->prj", returned, sine_table, preferred_element_type=jnp.float32)
    return jnp.stack([final_cos[0] - final_sin[1], final_cos[1] + final_sin[0]]).astype(
        jnp.bfloat16
    )


def per_device(launch, screens, distance, templates, send_table, send_counts):
    sections = lax.axis_size("layer")
    strips = lax.axis_size("strip")
    section_index = lax.axis_index("layer")
    fields = launch.shape[0]
    length = launch.shape[3]
    cosine_table, sine_table = fourier_tables(length)
    steps_total = fields + sections - 1

    def route(moment):
        entering = jnp.minimum(moment, fields - 1)
        leaving = moment - (sections - 1)
        finishing = leaving >= 0
        return (entering, leaving, finishing)

    def advance(moment, carry):
        arrived, finished = carry
        entering, leaving, finishing = route(moment)
        loaded = lax.dynamic_index_in_dim(launch, entering, 0, keepdims=False)
        current = jnp.where(section_index == 0, loaded, arrived)
        current = layer_step(current, screens[0], distance[0], cosine_table, sine_table, strips)
        keeping = jnp.logical_and(finishing, section_index == sections - 1)
        placed = lax.dynamic_update_index_in_dim(
            finished, current, jnp.clip(leaving, 0, fields - 1), 0
        )
        finished = jnp.where(keeping, placed, finished)
        arrived = passed_along(current, "layer", 1)
        return (arrived, finished)

    start_field = jnp.zeros(launch.shape[1:], jnp.bfloat16)
    carried = lax.fori_loop(0, steps_total, advance, (start_field, jnp.zeros_like(launch)))
    pupil = broadcast(carried[1], "layer", sections - 1)
    strip_rows = pupil.shape[2]
    blocks = pupil.reshape(fields, 2, strip_rows // SUB, SUB, length // SUB, SUB)
    blocks = blocks.transpose(2, 4, 0, 1, 3, 5).reshape(
        strip_rows // SUB * (length // SUB), fields * 2 * SUB * SUB
    )
    picks = send_table[0]
    live_counts = send_counts[0]
    slots_here = picks.shape[1]
    slot_number = section_index * slots_here + jnp.arange(slots_here, dtype=jnp.int32)
    live = slot_number[None, :] < live_counts[:, None]
    outgoing = jnp.where(live[:, :, None], blocks[picks], jnp.zeros((), jnp.bfloat16))
    big_table = spot_table(SUB)
    received = correlate_slots(
        lax.all_to_all(outgoing, "strip", split_axis=0, concat_axis=0, tiled=True),
        big_table,
        templates,
    )
    return (pupil, received[None])


def solution(mesh):
    placed = (
        P(None, None, "strip", None),
        P("layer", "strip", None),
        P("layer"),
        P(),
        P("strip", None, "layer"),
        P("strip", None),
    )
    return jax.shard_map(
        per_device,
        mesh=mesh,
        in_specs=placed,
        out_specs=(P(None, None, "strip", None), P("strip", None, "layer", None, None)),
        check_vma=False,
    )
```

profile of v0, /device:TPU:0, one launch (start us, length us, event | category | flops | bytes accessed | tf_op | source)
XLA Modules:
  0.0 1058.2 jit_solution(3029986198090210874)
XLA Ops:
  11.7 941.1 %while.20 = (s32[]{:T(128)}, bf16[2,128,1024]{2,1,0:T(8,128)(2,1)}, bf16[2,2,128,1024]{3,2,1,0:T(8,128)(2,1)S(1)}, pred[]{:T(512)}, bf16[2,2,128,1024]{3,2,1,0:T...) while((s32[]{:T(128)}, bf16[2,128,1024]{2,1,0:T(8,128)(2,1)}, ...), condition=%wide.region_1.2_spmd.clone.clone, body=%wide.region_0.1_spmd.clone.clone.sunk | while | flops 4437580800 | bytes 43016464 | solution.py:161
  13.3 16.3 %fusion.177 = f32[1024,2,128]{0,2,1:T(8,128)S(1)} fusion(bf16[1,128,1024]{2,1,0:T(8,128)(2,1)S(1)} %get-tuple-element.468, bf16[1,128,1024]{2,1,0:T(8,128)(2,1)S(1)} %get-tuple-element.469), kind=kOutput, calls=%fused_computation.24.clone.1 | convolution fusion | flops 553910272 | bytes 1572864 | tf_op jit(solution)/shard_map/while/body/eval_jaxpr/prj,jk->kpr/dot_general | solution.py:91
  29.5 16.1 %fusion.176 = f32[1024,2,128]{0,2,1:T(8,128)S(1)} fusion(bf16[1,128,1024]{2,1,0:T(8,128)(2,1)S(1)} %get-tuple-element.468, bf16[1,128,1024]{2,1,0:T(8,128)(2,1)S(1)} %get-tuple-element.469), kind=kOutput, calls=%fused_computation.27.clone.1 | convolution fusion | flops 553910272 | bytes 1572864 | tf_op jit(solution)/shard_map/while/body/eval_jaxpr/prj,jk->kpr/dot_general | solution.py:94
  46.1 21.7 %all_to_all.97 = bf16[8,128,2,128]{1,3,2,0:T(8,128)(2,1)S(1)} all-to-all(bf16[8,128,2,128]{1,3,2,0:T(8,128)(2,1)S(1)} %pad_maximum_fusion.20), channel_id=1, replica_groups=mesh['layer'=4,'strip'=8] {'strip'}, dimensions={0} | all-to-all | bytes 1048576 | tf_op jit(solution)/shard_map/while/body/eval_jaxpr/all_to_all | solution.py:104
  68.3 16.4 %fusion.179 = f32[1,128,2,1024]{3,1,2,0:T(8,128)S(1)} fusion(bf16[128,2,1024]{2,0,1:T(8,128)(2,1)S(1)} %reshape.566), kind=kOutput, calls=%fused_computation.28.clone.1 | convolution fusion | flops 553648128 | bytes 1572864 | tf_op jit(solution)/shard_map/while/body/eval_jaxpr/acpj,jk->acpk/dot_general | solution.py:106
  84.7 16.7 %fusion.180 = f32[1,128,2,1024]{3,1,2,0:T(8,128)S(1)} fusion(bf16[128,2,1024]{2,0,1:T(8,128)(2,1)S(1)} %reshape.566), kind=kOutput, calls=%fused_computation.25.clone.1 | convolution fusion | flops 553648128 | bytes 1572864 | tf_op jit(solution)/shard_map/while/body/eval_jaxpr/acpj,jk->acpk/dot_general | solution.py:105
  101.6 16.0 %fusion.183 = f32[1,128,2,1024]{3,1,2,0:T(8,128)S(1)} fusion(bf16[128,1,1024]{2,0,1:T(8,128)(2,1)S(1)} %get-tuple-element.472, bf16[128,1,1024]{2,0,1:T(8,128)(2,1)S(1)} %get-tuple-element.473), kind=kOutput, calls=%fused_computation.26.clone.1 | convolution fusion | flops 553910272 | bytes 1572864 | tf_op jit(solution)/shard_map/while/body/eval_jaxpr/acpj,kj->acpk/dot_general | solution.py:113
  117.6 16.1 %fusion.182 = f32[1,128,2,1024]{3,1,2,0:T(8,128)S(1)} fusion(bf16[128,1,1024]{2,0,1:T(8,128)(2,1)S(1)} %get-tuple-element.472, bf16[128,1,1024]{2,0,1:T(8,128)(2,1)S(1)} %get-tuple-element.473), kind=kOutput, calls=%fused_computation.29.clone.1 | convolution fusion | flops 553910272 | bytes 1572864 | tf_op jit(solution)/shard_map/while/body/eval_jaxpr/acpj,kj->acpk/dot_general | solution.py:114
  134.2 18.1 %all_to_all.98 = bf16[128,2,8,128]{3,0,1,2:T(8,128)(2,1)S(1)} all-to-all(bf16[128,2,8,128]{3,0,1,2:T(8,128)(2,1)S(1)} %pad_maximum_fusion.21), channel_id=1, replica_groups=mesh['layer'=4,'strip'=8] {'strip'}, dimensions={2} | all-to-all | bytes 1048576 | tf_op jit(solution)/shard_map/while/body/eval_jaxpr/all_to_all | solution.py:120
  152.9 16.4 %fusion.185 = f32[2,128,1024]{2,1,0:T(8,128)S(1)} fusion(bf16[1024,2,128]{0,2,1:T(8,128)(2,1)S(1)} %reshape.567), kind=kOutput, calls=%fused_computation.16.clone.1 | convolution fusion | flops 553648128 | bytes 1572864 | tf_op jit(solution)/shard_map/while/body/eval_jaxpr/kpr,kj->prj/dot_general | solution.py:125
  169.3 16.3 %fusion.186 = f32[2,128,1024]{2,1,0:T(8,128)S(1)} fusion(bf16[1024,2,128]{0,2,1:T(8,128)(2,1)S(1)} %reshape.567), kind=kOutput, calls=%fused_computation.20.clone.1 | convolution fusion | flops 553648128 | bytes 1572864 | tf_op jit(solution)/shard_map/while/body/eval_jaxpr/kpr,kj->prj/dot_general | solution.py:122
  190.4 9.8 collective-permute-done
  201.7 16.0 %fusion.177 = f32[1024,2,128]{0,2,1:T(8,128)S(1)} fusion(bf16[1,128,1024]{2,1,0:T(8,128)(2,1)S(1)} %get-tuple-element.468, bf16[1,128,1024]{2,1,0:T(8,128)(2,1)S(1)} %get-tuple-element.469), kind=kOutput, calls=%fused_computation.24.clone.1 | convolution fusion | flops 553910272 | bytes 1572864 | tf_op jit(solution)/shard_map/while/body/eval_jaxpr/prj,jk->kpr/dot_general | solution.py:91
  217.7 16.3 %fusion.176 = f32[1024,2,128]{0,2,1:T(8,128)S(1)} fusion(bf16[1,128,1024]{2,1,0:T(8,128)(2,1)S(1)} %get-tuple-element.468, bf16[1,128,1024]{2,1,0:T(8,128)(2,1)S(1)} %get-tuple-element.469), kind=kOutput, calls=%fused_computation.27.clone.1 | convolution fusion | flops 553910272 | bytes 1572864 | tf_op jit(solution)/shard_map/while/body/eval_jaxpr/prj,jk->kpr/dot_general | solution.py:94
  234.4 18.4 %all_to_all.97 = bf16[8,128,2,128]{1,3,2,0:T(8,128)(2,1)S(1)} all-to-all(bf16[8,128,2,128]{1,3,2,0:T(8,128)(2,1)S(1)} %pad_maximum_fusion.20), channel_id=1, replica_groups=mesh['layer'=4,'strip'=8] {'strip'}, dimensions={0} | all-to-all | bytes 1048576 | tf_op jit(solution)/shard_map/while/body/eval_jaxpr/all_to_all | solution.py:104
  253.4 16.4 %fusion.179 = f32[1,128,2,1024]{3,1,2,0:T(8,128)S(1)} fusion(bf16[128,2,1024]{2,0,1:T(8,128)(2,1)S(1)} %reshape.566), kind=kOutput, calls=%fused_computation.28.clone.1 | convolution fusion | flops 553648128 | bytes 1572864 | tf_op jit(solution)/shard_map/while/body/eval_jaxpr/acpj,jk->acpk/dot_general | solution.py:106
  269.8 16.5 %fusion.180 = f32[1,128,2,1024]{3,1,2,0:T(8,128)S(1)} fusion(bf16[128,2,1024]{2,0,1:T(8,128)(2,1)S(1)} %reshape.566), kind=kOutput, calls=%fused_computation.25.clone.1 | convolution fusion | flops 553648128 | bytes 1572864 | tf_op jit(solution)/shard_map/while/body/eval_jaxpr/acpj,jk->acpk/dot_general | solution.py:105
  286.5 16.2 %fusion.183 = f32[1,128,2,1024]{3,1,2,0:T(8,128)S(1)} fusion(bf16[128,1,1024]{2,0,1:T(8,128)(2,1)S(1)} %get-tuple-element.472, bf16[128,1,1024]{2,0,1:T(8,128)(2,1)S(1)} %get-tuple-element.473), kind=kOutput, calls=%fused_computation.26.clone.1 | convolution fusion | flops 553910272 | bytes 1572864 | tf_op jit(solution)/shard_map/while/body/eval_jaxpr/acpj,kj->acpk/dot_general | solution.py:113
  302.8 16.1 %fusion.182 = f32[1,128,2,1024]{3,1,2,0:T(8,128)S(1)} fusion(bf16[128,1,1024]{2,0,1:T(8,128)(2,1)S(1)} %get-tuple-element.472, bf16[128,1,1024]{2,0,1:T(8,128)(2,1)S(1)} %get-tuple-element.473), kind=kOutput, calls=%fused_computation.29.clone.1 | convolution fusion | flops 553910272 | bytes 1572864 | tf_op jit(solution)/shard_map/while/body/eval_jaxpr/acpj,kj->acpk/dot_general | solution.py:114
  319.3 17.9 %all_to_all.98 = bf16[128,2,8,128]{3,0,1,2:T(8,128)(2,1)S(1)} all-to-all(bf16[128,2,8,128]{3,0,1,2:T(8,128)(2,1)S(1)} %pad_maximum_fusion.21), channel_id=1, replica_groups=mesh['layer'=4,'strip'=8] {'strip'}, dimensions={2} | all-to-all | bytes 1048576 | tf_op jit(solution)/shard_map/while/body/eval_jaxpr/all_to_all | solution.py:120
  337.8 16.4 %fusion.185 = f32[2,128,1024]{2,1,0:T(8,128)S(1)} fusion(bf16[1024,2,128]{0,2,1:T(8,128)(2,1)S(1)} %reshape.567), kind=kOutput, calls=%fused_computation.16.clone.1 | convolution fusion | flops 553648128 | bytes 1572864 | tf_op jit(solution)/shard_map/while/body/eval_jaxpr/kpr,kj->prj/dot_general | solution.py:125
  354.2 16.3 %fusion.186 = f32[2,128,1024]{2,1,0:T(8,128)S(1)} fusion(bf16[1024,2,128]{0,2,1:T(8,128)(2,1)S(1)} %reshape.567), kind=kOutput, calls=%fused_computation.20.clone.1 | convolution fusion | flops 553648128 | bytes 1572864 | tf_op jit(solution)/shard_map/while/body/eval_jaxpr/kpr,kj->prj/dot_general | solution.py:122
  370.8 5.4 collective-permute-start
  376.4 9.8 collective-permute-done
  387.9 15.9 %fusion.177 = f32[1024,2,128]{0,2,1:T(8,128)S(1)} fusion(bf16[1,128,1024]{2,1,0:T(8,128)(2,1)S(1)} %get-tuple-element.468, bf16[1,128,1024]{2,1,0:T(8,128)(2,1)S(1)} %get-tuple-element.469), kind=kOutput, calls=%fused_computation.24.clone.1 | convolution fusion | flops 553910272 | bytes 1572864 | tf_op jit(solution)/shard_map/while/body/eval_jaxpr/prj,jk->kpr/dot_general | solution.py:91
  403.9 16.1 %fusion.176 = f32[1024,2,128]{0,2,1:T(8,128)S(1)} fusion(bf16[1,128,1024]{2,1,0:T(8,128)(2,1)S(1)} %get-tuple-element.468, bf16[1,128,1024]{2,1,0:T(8,128)(2,1)S(1)} %get-tuple-element.469), kind=kOutput, calls=%fused_computation.27.clone.1 | convolution fusion | flops 553910272 | bytes 1572864 | tf_op jit(solution)/shard_map/while/body/eval_jaxpr/prj,jk->kpr/dot_general | solution.py:94
  420.4 18.7 %all_to_all.97 = bf16[8,128,2,128]{1,3,2,0:T(8,128)(2,1)S(1)} all-to-all(bf16[8,128,2,128]{1,3,2,0:T(8,128)(2,1)S(1)} %pad_maximum_fusion.20), channel_id=1, replica_groups=mesh['layer'=4,'strip'=8] {'strip'}, dimensions={0} | all-to-all | bytes 1048576 | tf_op jit(solution)/shard_map/while/body/eval_jaxpr/all_to_all | solution.py:104
  439.7 16.4 %fusion.179 = f32[1,128,2,1024]{3,1,2,0:T(8,128)S(1)} fusion(bf16[128,2,1024]{2,0,1:T(8,128)(2,1)S(1)} %reshape.566), kind=kOutput, calls=%fused_computation.28.clone.1 | convolution fusion | flops 553648128 | bytes 1572864 | tf_op jit(solution)/shard_map/while/body/eval_jaxpr/acpj,jk->acpk/dot_general | solution.py:106
  456.1 16.4 %fusion.180 = f32[1,128,2,1024]{3,1,2,0:T(8,128)S(1)} fusion(bf16[128,2,1024]{2,0,1:T(8,128)(2,1)S(1)} %reshape.566), kind=kOutput, calls=%fused_computation.25.clone.1 | convolution fusion | flops 553648128 | bytes 1572864 | tf_op jit(solution)/shard_map/while/body/eval_jaxpr/acpj,jk->acpk/dot_general | solution.py:105
  472.7 16.0 %fusion.183 = f32[1,128,2,1024]{3,1,2,0:T(8,128)S(1)} fusion(bf16[128,1,1024]{2,0,1:T(8,128)(2,1)S(1)} %get-tuple-element.472, bf16[128,1,1024]{2,0,1:T(8,128)(2,1)S(1)} %get-tuple-element.473), kind=kOutput, calls=%fused_computation.26.clone.1 | convolution fusion | flops 553910272 | bytes 1572864 | tf_op jit(solution)/shard_map/while/body/eval_jaxpr/acpj,kj->acpk/dot_general | solution.py:113
  488.8 16.3 %fusion.182 = f32[1,128,2,1024]{3,1,2,0:T(8,128)S(1)} fusion(bf16[128,1,1024]{2,0,1:T(8,128)(2,1)S(1)} %get-tuple-element.472, bf16[128,1,1024]{2,0,1:T(8,128)(2,1)S(1)} %get-tuple-element.473), kind=kOutput, calls=%fused_computation.29.clone.1 | convolution fusion | flops 553910272 | bytes 1572864 | tf_op jit(solution)/shard_map/while/body/eval_jaxpr/acpj,kj->acpk/dot_general | solution.py:114
  505.6 17.9 %all_to_all.98 = bf16[128,2,8,128]{3,0,1,2:T(8,128)(2,1)S(1)} all-to-all(bf16[128,2,8,128]{3,0,1,2:T(8,128)(2,1)S(1)} %pad_maximum_fusion.21), channel_id=1, replica_groups=mesh['layer'=4,'strip'=8] {'strip'}, dimensions={2} | all-to-all | bytes 1048576 | tf_op jit(solution)/shard_map/while/body/eval_jaxpr/all_to_all | solution.py:120
  524.0 16.4 %fusion.185 = f32[2,128,1024]{2,1,0:T(8,128)S(1)} fusion(bf16[1024,2,128]{0,2,1:T(8,128)(2,1)S(1)} %reshape.567), kind=kOutput, calls=%fused_computation.16.clone.1 | convolution fusion | flops 553648128 | bytes 1572864 | tf_op jit(solution)/shard_map/while/body/eval_jaxpr/kpr,kj->prj/dot_general | solution.py:125
  540.4 16.3 %fusion.186 = f32[2,128,1024]{2,1,0:T(8,128)S(1)} fusion(bf16[1024,2,128]{0,2,1:T(8,128)(2,1)S(1)} %reshape.567), kind=kOutput, calls=%fused_computation.20.clone.1 | convolution fusion | flops 553648128 | bytes 1572864 | tf_op jit(solution)/shard_map/while/body/eval_jaxpr/kpr,kj->prj/dot_general | solution.py:122
  557.0 5.4 collective-permute-start
  562.6 9.8 collective-permute-done
  573.9 16.2 %fusion.177 = f32[1024,2,128]{0,2,1:T(8,128)S(1)} fusion(bf16[1,128,1024]{2,1,0:T(8,128)(2,1)S(1)} %get-tuple-element.468, bf16[1,128,1024]{2,1,0:T(8,128)(2,1)S(1)} %get-tuple-element.469), kind=kOutput, calls=%fused_computation.24.clone.1 | convolution fusion | flops 553910272 | bytes 1572864 | tf_op jit(solution)/shard_map/while/body/eval_jaxpr/prj,jk->kpr/dot_general | solution.py:91
  590.1 16.1 %fusion.176 = f32[1024,2,128]{0,2,1:T(8,128)S(1)} fusion(bf16[1,128,1024]{2,1,0:T(8,128)(2,1)S(1)} %get-tuple-element.468, bf16[1,128,1024]{2,1,0:T(8,128)(2,1)S(1)} %get-tuple-element.469), kind=kOutput, calls=%fused_computation.27.clone.1 | convolution fusion | flops 553910272 | bytes 1572864 | tf_op jit(solution)/shard_map/while/body/eval_jaxpr/prj,jk->kpr/dot_general | solution.py:94
  606.6 18.5 %all_to_all.97 = bf16[8,128,2,128]{1,3,2,0:T(8,128)(2,1)S(1)} all-to-all(bf16[8,128,2,128]{1,3,2,0:T(8,128)(2,1)S(1)} %pad_maximum_fusion.20), channel_id=1, replica_groups=mesh['layer'=4,'strip'=8] {'strip'}, dimensions={0} | all-to-all | bytes 1048576 | tf_op jit(solution)/shard_map/while/body/eval_jaxpr/all_to_all | solution.py:104
  625.7 16.4 %fusion.179 = f32[1,128,2,1024]{3,1,2,0:T(8,128)S(1)} fusion(bf16[128,2,1024]{2,0,1:T(8,128)(2,1)S(1)} %reshape.566), kind=kOutput, calls=%fused_computation.28.clone.1 | convolution fusion | flops 553648128 | bytes 1572864 | tf_op jit(solution)/shard_map/while/body/eval_jaxpr/acpj,jk->acpk/dot_general | solution.py:106
  642.1 16.7 %fusion.180 = f32[1,128,2,1024]{3,1,2,0:T(8,128)S(1)} fusion(bf16[128,2,1024]{2,0,1:T(8,128)(2,1)S(1)} %reshape.566), kind=kOutput, calls=%fused_computation.25.clone.1 | convolution fusion | flops 553648128 | bytes 1572864 | tf_op jit(solution)/shard_map/while/body/eval_jaxpr/acpj,jk->acpk/dot_general | solution.py:105
  659.0 16.0 %fusion.183 = f32[1,128,2,1024]{3,1,2,0:T(8,128)S(1)} fusion(bf16[128,1,1024]{2,0,1:T(8,128)(2,1)S(1)} %get-tuple-element.472, bf16[128,1,1024]{2,0,1:T(8,128)(2,1)S(1)} %get-tuple-element.473), kind=kOutput, calls=%fused_computation.26.clone.1 | convolution fusion | flops 553910272 | bytes 1572864 | tf_op jit(solution)/shard_map/while/body/eval_jaxpr/acpj,kj->acpk/dot_general | solution.py:113
  675.0 16.1 %fusion.182 = f32[1,128,2,1024]{3,1,2,0:T(8,128)S(1)} fusion(bf16[128,1,1024]{2,0,1:T(8,128)(2,1)S(1)} %get-tuple-element.472, bf16[128,1,1024]{2,0,1:T(8,128)(2,1)S(1)} %get-tuple-element.473), kind=kOutput, calls=%fused_computation.29.clone.1 | convolution fusion | flops 553910272 | bytes 1572864 | tf_op jit(solution)/shard_map/while/body/eval_jaxpr/acpj,kj->acpk/dot_general | solution.py:114
  691.6 18.1 %all_to_all.98 = bf16[128,2,8,128]{3,0,1,2:T(8,128)(2,1)S(1)} all-to-all(bf16[128,2,8,128]{3,0,1,2:T(8,128)(2,1)S(1)} %pad_maximum_fusion.21), channel_id=1, replica_groups=mesh['layer'=4,'strip'=8] {'strip'}, dimensions={2} | all-to-all | bytes 1048576 | tf_op jit(solution)/shard_map/while/body/eval_jaxpr/all_to_all | solution.py:120
  710.3 16.4 %fusion.185 = f32[2,128,1024]{2,1,0:T(8,128)S(1)} fusion(bf16[1024,2,128]{0,2,1:T(8,128)(2,1)S(1)} %reshape.567), kind=kOutput, calls=%fused_computation.16.clone.1 | convolution fusion | flops 553648128 | bytes 1572864 | tf_op jit(solution)/shard_map/while/body/eval_jaxpr/kpr,kj->prj/dot_general | solution.py:125
  726.7 16.3 %fusion.186 = f32[2,128,1024]{2,1,0:T(8,128)S(1)} fusion(bf16[1024,2,128]{0,2,1:T(8,128)(2,1)S(1)} %reshape.567), kind=kOutput, calls=%fused_computation.20.clone.1 | convolution fusion | flops 553648128 | bytes 1572864 | tf_op jit(solution)/shard_map/while/body/eval_jaxpr/kpr,kj->prj/dot_general | solution.py:122
  743.2 6.2 collective-permute-start
  749.6 9.8 collective-permute-done
  760.9 16.0 %fusion.177 = f32[1024,2,128]{0,2,1:T(8,128)S(1)} fusion(bf16[1,128,1024]{2,1,0:T(8,128)(2,1)S(1)} %get-tuple-element.468, bf16[1,128,1024]{2,1,0:T(8,128)(2,1)S(1)} %get-tuple-element.469), kind=kOutput, calls=%fused_computation.24.clone.1 | convolution fusion | flops 553910272 | bytes 1572864 | tf_op jit(solution)/shard_map/while/body/eval_jaxpr/prj,jk->kpr/dot_general | solution.py:91
  776.8 16.3 %fusion.176 = f32[1024,2,128]{0,2,1:T(8,128)S(1)} fusion(bf16[1,128,1024]{2,1,0:T(8,128)(2,1)S(1)} %get-tuple-element.468, bf16[1,128,1024]{2,1,0:T(8,128)(2,1)S(1)} %get-tuple-element.469), kind=kOutput, calls=%fused_computation.27.clone.1 | convolution fusion | flops 553910272 | bytes 1572864 | tf_op jit(solution)/shard_map/while/body/eval_jaxpr/prj,jk->kpr/dot_general | solution.py:94
  793.6 18.4 %all_to_all.97 = bf16[8,128,2,128]{1,3,2,0:T(8,128)(2,1)S(1)} all-to-all(bf16[8,128,2,128]{1,3,2,0:T(8,128)(2,1)S(1)} %pad_maximum_fusion.20), channel_id=1, replica_groups=mesh['layer'=4,'strip'=8] {'strip'}, dimensions={0} | all-to-all | bytes 1048576 | tf_op jit(solution)/shard_map/while/body/eval_jaxpr/all_to_all | solution.py:104
  812.6 16.4 %fusion.179 = f32[1,128,2,1024]{3,1,2,0:T(8,128)S(1)} fusion(bf16[128,2,1024]{2,0,1:T(8,128)(2,1)S(1)} %reshape.566), kind=kOutput, calls=%fused_computation.28.clone.1 | convolution fusion | flops 553648128 | bytes 1572864 | tf_op jit(solution)/shard_map/while/body/eval_jaxpr/acpj,jk->acpk/dot_general | solution.py:106
  829.0 16.5 %fusion.180 = f32[1,128,2,1024]{3,1,2,0:T(8,128)S(1)} fusion(bf16[128,2,1024]{2,0,1:T(8,128)(2,1)S(1)} %reshape.566), kind=kOutput, calls=%fused_computation.25.clone.1 | convolution fusion | flops 553648128 | bytes 1572864 | tf_op jit(solution)/shard_map/while/body/eval_jaxpr/acpj,jk->acpk/dot_general | solution.py:105
  845.7 16.2 %fusion.183 = f32[1,128,2,1024]{3,1,2,0:T(8,128)S(1)} fusion(bf16[128,1,1024]{2,0,1:T(8,128)(2,1)S(1)} %get-tuple-element.472, bf16[128,1,1024]{2,0,1:T(8,128)(2,1)S(1)} %get-tuple-element.473), kind=kOutput, calls=%fused_computation.26.clone.1 | convolution fusion | flops 553910272 | bytes 1572864 | tf_op jit(solution)/shard_map/while/body/eval_jaxpr/acpj,kj->acpk/dot_general | solution.py:113
  861.9 16.1 %fusion.182 = f32[1,128,2,1024]{3,1,2,0:T(8,128)S(1)} fusion(bf16[128,1,1024]{2,0,1:T(8,128)(2,1)S(1)} %get-tuple-element.472, bf16[128,1,1024]{2,0,1:T(8,128)(2,1)S(1)} %get-tuple-element.473), kind=kOutput, calls=%fused_computation.29.clone.1 | convolution fusion | flops 553910272 | bytes 1572864 | tf_op jit(solution)/shard_map/while/body/eval_jaxpr/acpj,kj->acpk/dot_general | solution.py:114
  878.5 17.9 %all_to_all.98 = bf16[128,2,8,128]{3,0,1,2:T(8,128)(2,1)S(1)} all-to-all(bf16[128,2,8,128]{3,0,1,2:T(8,128)(2,1)S(1)} %pad_maximum_fusion.21), channel_id=1, replica_groups=mesh['layer'=4,'strip'=8] {'strip'}, dimensions={2} | all-to-all | bytes 1048576 | tf_op jit(solution)/shard_map/while/body/eval_jaxpr/all_to_all | solution.py:120
  897.0 16.4 %fusion.185 = f32[2,128,1024]{2,1,0:T(8,128)S(1)} fusion(bf16[1024,2,128]{0,2,1:T(8,128)(2,1)S(1)} %reshape.567), kind=kOutput, calls=%fused_computation.16.clone.1 | convolution fusion | flops 553648128 | bytes 1572864 | tf_op jit(solution)/shard_map/while/body/eval_jaxpr/kpr,kj->prj/dot_general | solution.py:125
  913.4 16.3 %fusion.186 = f32[2,128,1024]{2,1,0:T(8,128)S(1)} fusion(bf16[1024,2,128]{0,2,1:T(8,128)(2,1)S(1)} %reshape.567), kind=kOutput, calls=%fused_computation.20.clone.1 | convolution fusion | flops 553648128 | bytes 1572864 | tf_op jit(solution)/shard_map/while/body/eval_jaxpr/kpr,kj->prj/dot_general | solution.py:122
  929.9 6.3 collective-permute-start
  936.5 9.8 collective-permute-done
  953.9 55.1 %all-reduce.2.cloned.1.call-done = bf16[2,2,128,1024]{3,2,1,0:T(8,128)(2,1)} async-done(((bf16[2,2,128,1024]{3,2,1,0:T(8,128)(2,1)}), bf16[2,2,128,1024]{3,2,1,0:T(8,128)(2,1)}) %all-reduce.2.cloned.1.call-update) | async-done | bytes 1048592 | tf_op jit(solution)/shard_map/psum | solution.py:19
  1009.0 9.1 reshape.537
  1018.1 7.1 copy.33
  1029.4 4.6 all-to-all-start.2
  (142 shorter events, 49.9 us)
Async XLA Ops:
  7.2 1042.3 %copy-start = (bf16[1024,16]{0,1:T(8,128)(2,1)S(1)}, bf16[1024,16]{0,1:T(8,128)(2,1)}, u32[]{:S(2)}) copy-start(bf16[1024,16]{0,1:T(8,128)(2,1)} %param.11) | copy-start | bytes 98308
  7.2 1001.8 %all-reduce.2.cloned.1.call-start = ((), (), s32[]{:S(2)}) async-start(), calls=%async_computation.3 | async-start | bytes 2097152 | tf_op jit(solution)/shard_map/psum | solution.py:19
  11.7 942.1 %copy-start.2 = (s32[1,8,1]{1,2,0:T(1,128)S(1)}, s32[1,8,1]{1,2,0:T(1,128)}, u32[]{:S(2)}) copy-start(s32[1,8,1]{1,2,0:T(1,128)} %param.12) | copy-start | bytes 100
  11.7 942.2 %copy-start.3 = (s32[1,8]{1,0:T(1,128)S(1)}, s32[1,8]{1,0:T(1,128)}, u32[]{:S(2)}) copy-start(s32[1,8]{1,0:T(1,128)} %param.13) | copy-start | bytes 100
  185.9 14.4 %collective-permute-start = (bf16[2,128,1024]{2,1,0:T(8,128)(2,1)S(1)}, bf16[2,128,1024]{2,1,0:T(8,128)(2,1)}, u32[]{:S(2)}, u32[]{:S(2)}) collective-permute-start(bf16[2,128,1024]{2,1,0:T(8,128)(2,1)S(1)} %pad_maximum_fusion.22), channel_id=1, source_target_pairs={{0,8},{8,16},{16,24},{1,9},{9,17},{17,25},{2,10},{10,18},{18,26},{... | collective-permute-start | bytes 1572872 | tf_op jit(solution)/shard_map/while/body/eval_jaxpr/ppermute | solution.py:14
  370.8 15.5 %collective-permute-start = (bf16[2,128,1024]{2,1,0:T(8,128)(2,1)S(1)}, bf16[2,128,1024]{2,1,0:T(8,128)(2,1)}, u32[]{:S(2)}, u32[]{:S(2)}) collective-permute-start(bf16[2,128,1024]{2,1,0:T(8,128)(2,1)S(1)} %pad_maximum_fusion.22), channel_id=1, source_target_pairs={{0,8},{8,16},{16,24},{1,9},{9,17},{17,25},{2,10},{10,18},{18,26},{... | collective-permute-start | bytes 1572872 | tf_op jit(solution)/shard_map/while/body/eval_jaxpr/ppermute | solution.py:14
  557.0 15.5 %collective-permute-start = (bf16[2,128,1024]{2,1,0:T(8,128)(2,1)S(1)}, bf16[2,128,1024]{2,1,0:T(8,128)(2,1)}, u32[]{:S(2)}, u32[]{:S(2)}) collective-permute-start(bf16[2,128,1024]{2,1,0:T(8,128)(2,1)S(1)} %pad_maximum_fusion.22), channel_id=1, source_target_pairs={{0,8},{8,16},{16,24},{1,9},{9,17},{17,25},{2,10},{10,18},{18,26},{... | collective-permute-start | bytes 1572872 | tf_op jit(solution)/shard_map/while/body/eval_jaxpr/ppermute | solution.py:14
  743.2 16.2 %collective-permute-start = (bf16[2,128,1024]{2,1,0:T(8,128)(2,1)S(1)}, bf16[2,128,1024]{2,1,0:T(8,128)(2,1)}, u32[]{:S(2)}, u32[]{:S(2)}) collective-permute-start(bf16[2,128,1024]{2,1,0:T(8,128)(2,1)S(1)} %pad_maximum_fusion.22), channel_id=1, source_target_pairs={{0,8},{8,16},{16,24},{1,9},{9,17},{17,25},{2,10},{10,18},{18,26},{... | collective-permute-start | bytes 1572872 | tf_op jit(solution)/shard_map/while/body/eval_jaxpr/ppermute | solution.py:14
  929.9 16.4 %collective-permute-start = (bf16[2,128,1024]{2,1,0:T(8,128)(2,1)S(1)}, bf16[2,128,1024]{2,1,0:T(8,128)(2,1)}, u32[]{:S(2)}, u32[]{:S(2)}) collective-permute-start(bf16[2,128,1024]{2,1,0:T(8,128)(2,1)S(1)} %pad_maximum_fusion.22), channel_id=1, source_target_pairs={{0,8},{8,16},{16,24},{1,9},{9,17},{17,25},{2,10},{10,18},{18,26},{... | collective-permute-start | bytes 1572872 | tf_op jit(solution)/shard_map/while/body/eval_jaxpr/ppermute | solution.py:14
  1029.4 18.4 %all-to-all-start.2 = ((bf16[8,2,512]{2,1,0:T(2,128)(2,1)}), bf16[8,2,512]{2,1,0:T(2,128)(2,1)S(1)}, u32[]{:S(2)}, u32[]{:S(2)}) async-start(bf16[8,2,512]{2,1,0:T(2,128)(2,1)} %reshape.562), calls=%async_computation.2 | async-start | bytes 32768 | tf_op jit(solution)/shard_map/all_to_all | solution.py:176
  1047.8 2.4 copy-start.1
Sparse Core Ops, SparseCore 0:
  953.9 55.0 all-reduce.1
where the time goes:
time: 1060 us
  matrix products  652 us (62%)
  blocking collectives  186 us (18%)
  waiting for transfers between devices  104 us (10%)
  local copies, waits for them, and re-layouts  41.6 us (4%)
  starting transfers between devices  32.4 us (3%)
  other arithmetic  18.4 us (2%)
  between operations  15 us (1%)
    all_to_all x5, blocking collectives, layer_step(): lax.all_to_all(spectrum, 'strip', split_axis=0, concat_axis=3, tiled=True)  95.7 us
    all_to_all x5, blocking collectives, layer_step(): lax.all_to_all(regrouped, 'strip', split_axis=2, concat_axis=0, tiled=True)  90.1 us
    dot_general x5, matrix products, layer_step(): jnp.einsum('acpj,jk->acpk', columns, cosine_table, preferred_element_type...  82.7 us
    dot_general x5, matrix products, layer_step(): jnp.einsum('acpj,jk->acpk', columns, sine_table, preferred_element_type=j...  82 us
    dot_general x5, matrix products, layer_step(): jnp.einsum('kpr,kj->prj', returned, sine_table, preferred_element_type=jn...  82 us
    dot_general x5, matrix products, layer_step(): jnp.einsum('kpr,kj->prj', returned, cosine_table, preferred_element_type=...  81.3 us
    dot_general x5, matrix products, layer_step(): jnp.einsum('prj,jk->kpr', screened, sine_table, preferred_element_type=jn...  80.9 us
    dot_general x5, matrix products, layer_step(): jnp.einsum('acpj,kj->acpk', phased, sine_table, preferred_element_type=jn...  80.8 us
  transfers between devices with their start and end apart: 7, of which 6 were waited for; matrix products, arithmetic and copies ran while one was open for 1% of the time, Pallas kernels for 0%

commit v1 on v0

v1 whole, which is shorter than its diff:
```python
import functools
import math

import jax
import jax.numpy as jnp
import numpy as np
from jax import lax
from jax.experimental import pallas as pl
from jax.experimental.pallas import tpu as pltpu
from jax.sharding import PartitionSpec as P

SUB = 16
F32 = jnp.float32
BF16 = jnp.bfloat16
MESH = pl.DeviceIdType.MESH


def cosine_half_table(length):
    k = np.arange(length // 2, dtype=np.int64)
    n = np.arange(length, dtype=np.int64)
    p = (k[:, None] * n[None, :]) % length
    p = np.minimum(p, length - p)
    return np.cos(2.0 * np.pi * p / length).astype(np.float32).astype(BF16)


def spot_table(subsize):
    spotsize = 2 * subsize
    outer = np.arange(spotsize)
    inner = np.arange(subsize)
    angles = (inner[:, None] * outer[None, :] % spotsize) * (2.0 * np.pi / spotsize)
    wave = (np.cos(angles) - 1j * np.sin(angles)) / math.sqrt(subsize)
    kron = wave[:, None, :, None] * wave[None, :, None, :]
    kron = kron.reshape(subsize * subsize, spotsize * spotsize)
    upper = np.concatenate([kron.real, kron.imag], axis=1)
    lower = np.concatenate([-kron.imag, kron.real], axis=1)
    return np.concatenate([upper, lower], axis=0).astype(np.float32).astype(BF16)


def kernel_line(distance_value, length):
    half = length // 2
    counter = jnp.arange(half + 1, dtype=jnp.int32).astype(F32)
    phases = -distance_value * math.pi * counter * counter / float(length * length)
    h = jnp.stack([jnp.cos(phases), jnp.sin(phases)])
    weight = jnp.where(counter == 0.0, 1.0, 2.0) / length
    folded = (h * weight)[:, :half]
    high = folded.astype(BF16)
    low = (folded - high.astype(F32)).astype(BF16)
    table = jnp.asarray(cosine_half_table(length))
    parts = jnp.dot(jnp.concatenate([high, low]), table, preferred_element_type=F32)
    sign = (1 - 2 * (jnp.arange(length, dtype=jnp.int32) % 2)).astype(F32) / length
    line = parts[:2] + parts[2:] + h[:, half:] * sign
    return jnp.concatenate([line, jnp.zeros((6, length), F32)])


def sincos(x):
    y = 0.5 * x
    z = y * y
    s = -1.0 / 39916800.0
    for c in (1.0 / 362880.0, -1.0 / 5040.0, 1.0 / 120.0, -1.0 / 6.0, 1.0):
        s = s * z + c
    s = s * y
    c0 = 1.0 / 479001600.0
    for c in (-1.0 / 3628800.0, 1.0 / 40320.0, -1.0 / 720.0, 1.0 / 24.0, -0.5, 1.0):
        c0 = c0 * z + c
    return 2.0 * s * c0, 1.0 - 2.0 * s * s


def propagate_kernel(
    layers, strips, launch_ref, scr_ref, scrt_ref, g_ref, out_ref,
    gall, gmat, srow, scol, sendbuf, recvbuf, slab, swapped, mid,
    gsend, grecv, ssend, srecv, xsend, xrecv, osend, orecv,
):
    count = layers * strips
    length = launch_ref.shape[-1]
    lines = launch_ref.shape[-2]
    wide = 4 * lines
    sec = lax.axis_index("layer")
    strip = lax.axis_index("strip")
    me = strip * layers + sec

    barrier = pltpu.get_barrier_semaphore()

    def greet(k, _):
        peer = lax.rem(me + k, count)
        pl.semaphore_signal(
            barrier, inc=1, device_id=(lax.rem(peer, layers), peer // layers), device_id_type=MESH
        )
        return 0

    lax.fori_loop(1, count, greet, 0)
    pl.semaphore_wait(barrier, count - 1)

    def remote(src, dst, ssem, rsem, a, s):
        return pltpu.make_async_remote_copy(
            src_ref=src, dst_ref=dst, send_sem=ssem, recv_sem=rsem,
            device_id=(a, s), device_id_type=MESH,
        )

    for k in range(1, layers):
        a = lax.rem(sec + k, layers)
        remote(g_ref, gall.at[sec], gsend, grecv.at[sec], a, strip).start()
    for lay in range(layers):
        if lay % 2 == 0:
            @pl.when(sec == lay)
            def _(lay=lay):
                for k in range(1, layers):
                    a = lax.rem(sec + k, layers)
                    remote(scr_ref.at[a], srow.at[lay // 2], ssend, srecv.at[lay], a, strip).start()
                srow[lay // 2] = scr_ref[lay]
        else:
            @pl.when(sec == lay)
            def _(lay=lay):
                def give(k, _):
                    peer = lax.rem(me + k, count)
                    remote(
                        scrt_ref.at[peer], scol.at[lay // 2, strip], ssend, srecv.at[lay],
                        lax.rem(peer, layers), peer // layers,
                    ).start()
                    return 0

                lax.fori_loop(1, count, give, 0)
                scol[lay // 2, strip] = scrt_ref[me]
    gall[sec] = g_ref[...]

    def build(lay):
        @pl.when(sec != lay)
        def _():
            remote(g_ref, gall.at[lay], gsend, grecv.at[lay], sec, strip).wait_recv()

        band = 128
        for part in range(2):
            row = gall[lay, part:part + 1, :]
            base = pltpu.roll(
                jnp.broadcast_to(row, (band, length)), 0, axis=1, stride=1, stride_axis=0
            ).astype(BF16)
            for b in range(length // band):
                at = band * b
                if b:
                    gmat[lay, part, at:at + band, 0:at] = base[:, length - at:]
                gmat[lay, part, at:at + band, at:] = base[:, :length - at]

    def screen_of(lay):
        if lay % 2 == 0:
            @pl.when(sec != lay)
            def _():
                remote(scr_ref.at[0], srow.at[lay // 2], ssend, srecv.at[lay], sec, strip).wait_recv()
            return sincos(srow[lay // 2])

        @pl.when(sec != lay)
        def _():
            whole = scol.at[lay // 2]
            remote(whole, whole, ssend, srecv.at[lay], sec, strip).wait_recv()

        @pl.when(sec == lay)
        def _():
            most = scol.at[lay // 2, pl.ds(0, strips - 1)]
            remote(most, most, ssend, srecv.at[lay], sec, strip).wait_recv()

        theta = jnp.concatenate([scol[lay // 2, s] for s in range(strips)], axis=1)
        return sincos(theta)

    def put(fc, value):
        rounded = value.astype(BF16)
        slab[fc * lines:(fc + 1) * lines, :] = rounded
        other = fc ^ 1
        swapped[other * lines:(other + 1) * lines, :] = rounded if fc % 2 == 0 else -rounded

    def screened(lay, load):
        sine, cosine = screen_of(lay)
        for f in range(2):
            re = load(2 * f)
            im = load(2 * f + 1)
            put(2 * f, re * cosine - im * sine)
            put(2 * f + 1, re * sine + im * cosine)

    block = 256

    def across(lay, step):
        def body(b, _):
            at = pl.ds(pl.multiple_of(b * block, block), block)
            dims = (((1,), (1,)), ((), ()))
            total = lax.dot_general(
                gmat[lay, 0, at, :], slab[...], dims, preferred_element_type=F32
            ) + lax.dot_general(
                gmat[lay, 1, at, :], swapped[...], dims, preferred_element_type=F32
            )
            per = block // lines
            sendbuf[step, pl.ds(b * per, per)] = total.reshape(per, lines, wide).astype(BF16)
            return 0

        lax.fori_loop(0, length // block, body, 0)

        def give(k, _):
            peer = lax.rem(me + k, count)
            remote(
                sendbuf.at[step, peer], recvbuf.at[step, me], xsend.at[step], xrecv.at[step],
                lax.rem(peer, layers), peer // layers,
            ).start()
            return 0

        lax.fori_loop(1, count, give, 0)
        recvbuf[step, me] = sendbuf[step, me]

    def arrived(step):
        most = recvbuf.at[step, pl.ds(0, count - 1)]
        remote(most, most, xsend.at[step], xrecv.at[step], sec, strip).wait_recv()
        if wide == 128:
            lane = lax.broadcasted_iota(jnp.int32, (lines, wide), 1) // lines
            for g in range(count // 4):
                pieces = [recvbuf[step, 4 * g + q].astype(F32) for q in range(4)]
                for fc in range(4):
                    out = None
                    for q in range(4):
                        shift = ((q - fc) * lines) % wide
                        moved = pltpu.roll(pieces[q], shift, axis=1) if shift else pieces[q]
                        out = moved if out is None else jnp.where(lane == q, moved, out)
                    rounded = out.astype(BF16)
                    at = slice(g * wide, (g + 1) * wide)
                    slab[fc * lines:(fc + 1) * lines, at] = rounded
                    other = fc ^ 1
                    swapped[other * lines:(other + 1) * lines, at] = (
                        rounded if fc % 2 == 0 else -rounded
                    )
        else:
            for fc in range(4):
                put(fc, jnp.concatenate(
                    [
                        recvbuf[step, d].astype(F32)[:, fc * lines:(fc + 1) * lines]
                        for d in range(count)
                    ],
                    axis=1,
                ))

    def along(lay):
        def body(b, _):
            at = pl.ds(pl.multiple_of(b * block, block), block)
            mid[:, at] = jnp.dot(
                slab[...], gmat[lay, 0, :, at], preferred_element_type=F32
            ) + jnp.dot(swapped[...], gmat[lay, 1, :, at], preferred_element_type=F32)
            return 0

        lax.fori_loop(0, length // block, body, 0)

    build(0)
    screened(0, lambda fc: launch_ref[fc, sec].astype(F32))
    across(0, 0)
    for lay in range(1, layers):
        build(lay)
    for lay in range(1, layers):
        arrived(lay - 1)
        along(lay - 1)
        screened(lay, lambda fc: mid[fc * lines:(fc + 1) * lines, :])
        across(lay, lay)
    arrived(layers - 1)
    along(layers - 1)
    for fc in range(4):
        out_ref[sec, fc] = mid[fc * lines:(fc + 1) * lines, :].astype(BF16)
    for k in range(1, layers):
        a = lax.rem(sec + k, layers)
        remote(out_ref.at[sec], out_ref.at[sec], osend, orecv, a, strip).start()
    most = out_ref.at[pl.ds(0, layers - 1)]
    remote(most, most, osend, orecv, sec, strip).wait()
    for k in range(1, layers):
        remote(g_ref, gall.at[sec], gsend, grecv.at[sec], sec, strip).wait_send()
    for lay in range(layers):
        @pl.when(sec == lay)
        def _(lay=lay):
            if lay % 2 == 0:
                some = scr_ref.at[pl.ds(0, layers - 1)]
            else:
                some = scrt_ref.at[pl.ds(0, count - 1)]
            remote(some, some, ssend, srecv.at[lay], sec, strip).wait_send()
    for step in range(layers):
        most = sendbuf.at[step, pl.ds(0, count - 1)]
        remote(most, most, xsend.at[step], xrecv.at[step], sec, strip).wait_send()


def propagate(launch, screens, line, layers, strips):
    rows, length = launch.shape[2:]
    lines = rows // layers
    count = layers * strips
    vmem = pl.BlockSpec(memory_space=pltpu.VMEM)
    dma = pltpu.SemaphoreType.DMA
    screen = screens[0]
    return pl.pallas_call(
        functools.partial(propagate_kernel, layers, strips),
        out_shape=jax.ShapeDtypeStruct((layers, 4, lines, length), BF16),
        in_specs=[vmem] * 4,
        out_specs=vmem,
        scratch_shapes=[
            pltpu.VMEM((layers, 8, length), F32),
            pltpu.VMEM((layers, 2, length, length), BF16),
            pltpu.VMEM((layers // 2, lines, length), F32),
            pltpu.VMEM((layers // 2, strips, lines, rows), F32),
            pltpu.VMEM((layers, count, lines, 4 * lines), BF16),
            pltpu.VMEM((layers, count, lines, 4 * lines), BF16),
            pltpu.VMEM((4 * lines, length), BF16),
            pltpu.VMEM((4 * lines, length), BF16),
            pltpu.VMEM((4 * lines, length), F32),
            dma, dma((layers,)), dma, dma((layers,)), dma((layers,)), dma((layers,)), dma, dma,
        ],
        compiler_params=pltpu.CompilerParams(
            collective_id=0, has_side_effects=True, vmem_limit_bytes=56 << 20
        ),
        name="propagate",
    )(
        launch.reshape(4, layers, lines, length),
        screen.reshape(layers, lines, length),
        screen.T.reshape(count, lines, rows),
        line,
    )


def per_device(launch, screens, distance, templates, send_table, send_counts):
    layers = lax.axis_size("layer")
    strips = lax.axis_size("strip")
    sec = lax.axis_index("layer")
    fields = launch.shape[0]
    rows, length = launch.shape[2:]
    line = kernel_line(distance[0], length)
    done = propagate(launch, screens, line, layers, strips)
    pupil = done.transpose(1, 0, 2, 3).reshape(fields, 2, rows, length)
    side = length // SUB
    picks = send_table[0, :, 0]
    blocks = jnp.stack([
        lax.dynamic_slice(
            pupil,
            (0, 0, picks[o] // side * SUB, picks[o] % side * SUB),
            (fields, 2, SUB, SUB),
        )
        for o in range(strips)
    ])
    flat = blocks.reshape(strips * fields, 2 * SUB * SUB)
    table = jnp.asarray(spot_table(SUB))
    pixels = templates.shape[0]
    spot = jnp.dot(flat, table, preferred_element_type=F32)
    intensity = (spot[:, :pixels] ** 2 + spot[:, pixels:] ** 2).astype(BF16)
    result = jnp.dot(intensity, templates, preferred_element_type=F32)
    result = result.reshape(strips, fields, templates.shape[1])
    live = sec < send_counts[0]
    result = jnp.where(live[:, None, None], result, 0.0)
    received = lax.all_to_all(result, "strip", split_axis=0, concat_axis=0, tiled=True)
    return (pupil, received[None, :, None])


def solution(mesh):
    placed = (
        P(None, None, "strip", None),
        P("layer", "strip", None),
        P("layer"),
        P(),
        P("strip", None, "layer"),
        P("strip", None),
    )
    return jax.shard_map(
        per_device,
        mesh=mesh,
        in_specs=placed,
        out_specs=(P(None, None, "strip", None), P("strip", None, "layer", None, None)),
        check_vma=False,
    )
```

time: 1060 us -> 121 us (0.11)
  matrix products: 652 us -> 1.99 us
  blocking collectives: 186 us -> 11.5 us
  waiting for transfers between devices: 104 us -> 0 us
  Pallas kernels: 0 us -> 77.2 us
  local copies, waits for them, and re-layouts: 41.6 us -> 7.19 us
  starting transfers between devices: 32.4 us -> 0 us
  other arithmetic: 18.4 us -> 0.4 us
    dot_general x42 -> x3, matrix products: 652 us -> 1.99 us  [the longest x1 1.48 us: kernel_line(): jnp.dot(jnp.concatenate([high, low]), table, preferred_element_type=F32)]
    all_to_all x10 -> x1, blocking collectives: 186 us -> 11.5 us  [per_device(): lax.all_to_all(result, 'strip', split_axis=0, concat_axis=0, tiled=True)]
    pallas_call x0 -> x1, Pallas kernels: none -> 77.2 us  [propagate(): pl.pallas_call(functools.partial(propagate_kernel, layers, strips), out_s...]
    psum x1 -> x0, waiting for transfers between devices: 55.1 us -> none  [broadcast(): return lax.psum(jnp.where(mine, x, jnp.zeros_like(x)), axis)]
    ppermute x5 -> x0, waiting for transfers between devices: 49 us -> none  [passed_along(): lax.ppermute(value, axis, [(source, source + steps) for source in range(f...]
    ppermute x5 -> x0, starting transfers between devices: 27.7 us -> none  [passed_along(): lax.ppermute(value, axis, [(source, source + steps) for source in range(f...]
    another operation x29 -> x1, local copies, waits for them, and re-layouts: 12.1 us -> 0.1 us  [per_device(): jnp.stack([lax.dynamic_slice(pupil, (0, 0, picks[o] // side * SUB, picks[...]
    reshape x8 -> x1, local copies, waits for them, and re-layouts: 12 us -> 0.18 us  [per_device(): flat = blocks.reshape(strips * fields, 2 * SUB * SUB)]
  transfers between devices with their start and end apart: 7 -> 0, of which waited for: 6 -> 0; matrix products, arithmetic and copies ran while one was open for 1% -> 0% of each run, Pallas kernels for 0% -> 0%
where the time goes in v1:
time: 121 us; the launch traced here: 120 us
  Pallas kernels  77.2 us (64%)
  between operations  21.8 us (18%)
  blocking collectives  11.5 us (10%)
  local copies, waits for them, and re-layouts  7.19 us (6%)
  matrix products  1.99 us (2%)
    pallas_call x1, Pallas kernels, propagate(): pl.pallas_call(functools.partial(propagate_kernel, layers, strips), out_s...  77.2 us
    all_to_all x1, blocking collectives, per_device(): lax.all_to_all(result, 'strip', split_axis=0, concat_axis=0, tiled=True)  11.5 us

profile of v1, /device:TPU:0, one launch (start us, length us, event | category | flops | bytes accessed | tf_op | source)
XLA Modules:
  0.0 120.0 jit_solution(7433697487522553404)
XLA Ops:
  0.6 0.0 copy-start
  0.7 1.6 %fusion.20 = (s32[1,1,1]{1,2,0:T(1,128)}, s32[1,1,1]{1,2,0:T(1,128)}, s32[1,1,1]{1,2,0:T(1,128)}, s32[1,1,1]{1,2,0:T(1,128)}, s32[1,1,1]{1,2,0:T(1,128)}, /*inde...) fusion(s32[1,8,1]{1,2,0:T(1,128)} %param.12), kind=kLoop, calls=%fused_computation.42 | loop fusion | bytes 64 | tf_op jit(solution)/shard_map/slice | solution.py:328
  22.6 2.0 %copy.15 = f32[1024,128]{1,0:T(8,128)} copy(f32[1024,128]{0,1:T(8,128)} %bitcast.44) | data formatting | bytes 1048576 | tf_op jit(solution)/shard_map/transpose | solution.py:309
  25.3 0.1 fusion.16
  25.4 0.1 fusion.18
  25.6 1.5 %fusion.14 = f32[4,1024]{1,0:T(4,128)S(1)} fusion(bf16[512,1024]{1,0:T(8,128)(2,1)} %constant.154.clone, bf16[2,512]{1,0:T(2,128)(2,1)S(1)} %get-tuple-element.2, bf16[2,512]{1,0:T(2,128)(2,1)S(1)} %get-tuple-element.3), kind=kOutput, calls=%fused_computation.33 | convolution fusion | flops 4202496 | bytes 1069056 | tf_op jit(solution)/shard_map/dot_general | solution.py:49
  27.0 0.1 fusion.4
  27.1 0.6 concatenate.7.g_ref
  27.7 0.0 copy-start.1
  27.7 77.2 %propagate.1 = bf16[4,4,32,1024]{3,2,1,0:T(8,128)(2,1)} custom-call(bf16[4,4,32,1024]{3,2,1,0:T(8,128)(2,1)} %bitcast.56, f32[4,32,1024]{2,1,0:T(8,128)} %bitcast.45, f32[32,32,128]{2,1,0:T(8,128)} %bitcast.46, f32[8,1024]{1,0:T(8,128)} %concatenate.7.g_ref), custom_call_target="tpu_custom_call" | custom-call | tf_op jit(solution)/shard_map/propagate/pallas_call | solution.py:285
  104.9 0.0 copy-start.3
  104.9 1.3 %copy.16 = bf16[4,4,32,1024]{3,2,1,0:T(8,128)(2,1)S(1)} copy(bf16[4,4,32,1024]{3,2,0,1:T(8,128)(2,1)} %bitcast.43) | data formatting | bytes 2097152 | tf_op jit(solution)/shard_map/transpose | solution.py:322
  106.3 0.0 copy-start.2
  106.4 0.1 constant_dynamic-update-slice_fusion.7
  106.5 0.1 constant_dynamic-update-slice_fusion.6
  106.5 0.1 constant_dynamic-update-slice_fusion.5
  106.6 0.1 constant_dynamic-update-slice_fusion.4
  106.7 0.1 constant_dynamic-update-slice_fusion.3
  106.8 0.1 constant_dynamic-update-slice_fusion.2
  106.9 0.1 constant_dynamic-update-slice_fusion.1
  107.0 0.1 constant_dynamic-update-slice_fusion
  107.1 0.2 reshape.89
  107.3 0.0 copy-done.1
  107.3 0.4 fusion.21
  107.7 0.0 copy-done
  107.7 0.1 fusion.2
  107.8 0.0 copy-done.3
  107.9 0.1 broadcast_select_fusion
  107.9 11.5 %all_to_all.5 = f32[8,2,16]{2,1,0:T(2,128)S(1)} all-to-all(f32[8,2,16]{2,1,0:T(2,128)S(1)} %broadcast_select_fusion), channel_id=1, replica_groups=mesh['layer'=4,'strip'=8] {'strip'}, dimensions={0} | all-to-all | bytes 2048 | tf_op jit(solution)/shard_map/all_to_all | solution.py:342
  119.4 0.6 copy.26
  120.0 0.0 copy-done.2
  (5 shorter events, 0.0 us)
Async XLA Ops:
  0.6 107.1 %copy-start = (bf16[1024,16]{0,1:T(8,128)(2,1)S(1)}, bf16[1024,16]{0,1:T(8,128)(2,1)}, u32[]{:S(2)}) copy-start(bf16[1024,16]{0,1:T(8,128)(2,1)} %param.11) | copy-start | bytes 98308
  27.7 79.6 %copy-start.1 = (bf16[512,2048]{1,0:T(8,128)(2,1)S(1)}, bf16[512,2048]{1,0:T(8,128)(2,1)}, u32[]{:S(2)}) copy-start(bf16[512,2048]{1,0:T(8,128)(2,1)} %constant.155.clone) | copy-start | bytes 6291460
  104.9 2.9 %copy-start.3 = (s32[1,8]{1,0:T(1,128)S(1)}, s32[1,8]{1,0:T(1,128)}, u32[]{:S(2)}) copy-start(s32[1,8]{1,0:T(1,128)} %param.13) | copy-start | bytes 100
  106.3 13.8 %copy-start.2 = (bf16[4,4,32,1024]{3,2,1,0:T(8,128)(2,1)}, bf16[4,4,32,1024]{3,2,1,0:T(8,128)(2,1)S(1)}, u32[]{:S(2)}) copy-start(bf16[4,4,32,1024]{3,2,1,0:T(8,128)(2,1)S(1)} %copy.16) | copy-start | bytes 3145732

commit v2 on v1

--- a/solution.py
+++ b/solution.py
@@ -311,6 +311,68 @@
     )
 
 
+def gather_kernel(side, picks_ref, pupil_ref, out_ref):
+    for o in range(out_ref.shape[0]):
+        pick = picks_ref[o]
+        top = pl.multiple_of(pick // side * SUB, SUB)
+        left = pick % side * SUB
+        tile = pl.multiple_of(left // 128 * 128, 128)
+        shift = (128 - left % 128) % 128
+        for part in range(4):
+            rows = pupil_ref[part, pl.ds(top, SUB), pl.ds(tile, 128)].astype(F32)
+            out_ref[o, part] = pltpu.roll(rows, shift, axis=1)[:, :SUB].astype(BF16)
+
+
+def gather_blocks(pupil, picks):
+    vmem = pl.BlockSpec(memory_space=pltpu.VMEM)
+    return pl.pallas_call(
+        functools.partial(gather_kernel, pupil.shape[-1] // SUB),
+        out_shape=jax.ShapeDtypeStruct((picks.shape[0], 4, SUB, SUB), BF16),
+        in_specs=[pl.BlockSpec(memory_space=pltpu.SMEM), vmem],
+        out_specs=vmem,
+        name="gather",
+    )(picks, pupil)
+
+
+def swap_kernel(strips, in_ref, out_ref, send, recv):
+    sec = lax.axis_index("layer")
+    strip = lax.axis_index("strip")
+    barrier = pltpu.get_barrier_semaphore()
+    for k in range(1, strips):
+        pl.semaphore_signal(
+            barrier, inc=1, device_id=(sec, lax.rem(strip + k, strips)), device_id_type=MESH
+        )
+    pl.semaphore_wait(barrier, strips - 1)
+    for k in range(1, strips):
+        peer = lax.rem(strip + k, strips)
+        pltpu.make_async_remote_copy(
+            src_ref=in_ref.at[peer], dst_ref=out_ref.at[strip], send_sem=send, recv_sem=recv,
+            device_id=(sec, peer), device_id_type=MESH,
+        ).start()
+    out_ref[strip] = in_ref[strip]
+    most = out_ref.at[pl.ds(0, strips - 1)]
+    pltpu.make_async_remote_copy(
+        src_ref=most, dst_ref=most, send_sem=send, recv_sem=recv,
+        device_id=(sec, strip), device_id_type=MESH,
+    ).wait()
+
+
+def swap_strips(result, strips):
+    fields, channels = result.shape[1:]
+    vmem = pl.BlockSpec(memory_space=pltpu.VMEM)
+    dma = pltpu.SemaphoreType.DMA
+    out = pl.pallas_call(
+        functools.partial(swap_kernel, strips),
+        out_shape=jax.ShapeDtypeStruct((strips, 8, 128), F32),
+        in_specs=[vmem],
+        out_specs=vmem,
+        scratch_shapes=[dma, dma],
+        compiler_params=pltpu.CompilerParams(collective_id=1, has_side_effects=True),
+        name="swap",
+    )(jnp.pad(result, ((0, 0), (0, 8 - fields), (0, 128 - channels))))
+    return out[:, :fields, :channels]
+
+
 def per_device(launch, screens, distance, templates, send_table, send_counts):
     layers = lax.axis_size("layer")
     strips = lax.axis_size("strip")
@@ -321,15 +383,7 @@
     done = propagate(launch, screens, line, layers, strips)
     pupil = done.transpose(1, 0, 2, 3).reshape(fields, 2, rows, length)
     side = length // SUB
-    picks = send_table[0, :, 0]
-    blocks = jnp.stack([
-        lax.dynamic_slice(
-            pupil,
-            (0, 0, picks[o] // side * SUB, picks[o] % side * SUB),
-            (fields, 2, SUB, SUB),
-        )
-        for o in range(strips)
-    ])
+    blocks = gather_blocks(pupil.reshape(2 * fields, rows, length), send_table.reshape(strips))
     flat = blocks.reshape(strips * fields, 2 * SUB * SUB)
     table = jnp.asarray(spot_table(SUB))
     pixels = templates.shape[0]
@@ -339,7 +393,7 @@
     result = result.reshape(strips, fields, templates.shape[1])
     live = sec < send_counts[0]
     result = jnp.where(live[:, None, None], result, 0.0)
-    received = lax.all_to_all(result, "strip", split_axis=0, concat_axis=0, tiled=True)
+    received = swap_strips(result, strips)
     return (pupil, received[None, :, None])
 
 

time: 121 us -> 99.9 us (0.83)
  between operations: 21.8 us -> 1.36 us
  blocking collectives: 11.5 us -> 0 us
  Pallas kernels: 77.2 us -> 87.5 us
    all_to_all x1 -> x0, blocking collectives: 11.5 us -> none  [per_device(): lax.all_to_all(result, 'strip', split_axis=0, concat_axis=0, tiled=True)]
    pallas_call x0 -> x2, Pallas kernels: none -> 10.5 us  [the longest x1 8.4 us: swap_strips(): pl.pallas_call(functools.partial(swap_kernel, strips), out_shape=jax.Shap...]
    slice x1 -> x0, local copies, waits for them, and re-layouts: 1.64 us -> none  [per_device(): picks[o] // side * SUB]
where the time goes in v2:
time: 99.9 us; the launch traced here: 99.5 us
  Pallas kernels  87.5 us (88%)
  local copies, waits for them, and re-layouts  8.2 us (8%)
  matrix products  1.99 us (2%)
  between operations  1.36 us (1%)
    pallas_call x1, Pallas kernels, propagate(): pl.pallas_call(functools.partial(propagate_kernel, layers, strips), out_s...  77 us
    pallas_call x1, Pallas kernels, swap_strips(): pl.pallas_call(functools.partial(swap_kernel, strips), out_shape=jax.Shap...  8.4 us
    transpose x1, local copies, waits for them, and re-layouts, per_device(): pupil = done.transpose(1, 0, 2, 3).reshape(fields, 2, rows, length)  2.44 us
    pallas_call x1, Pallas kernels, gather_blocks(): pl.pallas_call(functools.partial(gather_kernel, pupil.shape[-1] // SUB),...  2.09 us
    transpose x1, local copies, waits for them, and re-layouts, propagate(): screen.T.reshape(count, lines, rows)  2.03 us

profile of v2, /device:TPU:0, one launch (start us, length us, event | category | flops | bytes accessed | tf_op | source)
XLA Modules:
  0.0 99.5 jit_solution(16916695029315701741)
XLA Ops:
  0.6 0.0 copy-start
  1.3 0.1 fusion.16
  1.4 1.5 %fusion.14 = f32[4,1024]{1,0:T(4,128)S(1)} fusion(bf16[512,1024]{1,0:T(8,128)(2,1)} %constant.48.clone, bf16[2,512]{1,0:T(2,128)(2,1)S(1)} %get-tuple-element.10, bf16[2,512]{1,0:T(2,128)(2,1)S(1)} %get-tuple-element.11), kind=kOutput, calls=%fused_computation.26 | convolution fusion | flops 4202496 | bytes 1069056 | tf_op jit(solution)/shard_map/dot_general | solution.py:49
  2.9 0.1 fusion.18
  3.0 0.1 fusion.4
  3.1 0.6 concatenate.7.g_ref
  3.8 2.0 %copy.21 = f32[1024,128]{1,0:T(8,128)} copy(f32[1024,128]{0,1:T(8,128)} %bitcast.27) | data formatting | bytes 1048576 | tf_op jit(solution)/shard_map/transpose | solution.py:309
  5.8 77.0 %propagate.1 = bf16[4,4,32,1024]{3,2,1,0:T(8,128)(2,1)} custom-call(bf16[4,4,32,1024]{3,2,1,0:T(8,128)(2,1)} %bitcast.30, f32[4,32,1024]{2,1,0:T(8,128)} %bitcast.28, f32[32,32,128]{2,1,0:T(8,128)} %bitcast.29, f32[8,1024]{1,0:T(8,128)} %concatenate.7.g_ref), custom_call_target="tpu_custom_call" | custom-call | tf_op jit(solution)/shard_map/propagate/pallas_call | solution.py:285
  82.8 0.0 copy-start.1
  82.8 2.4 %copy.22 = bf16[4,4,32,1024]{3,2,1,0:T(8,128)(2,1)} copy(bf16[4,4,32,1024]{3,2,0,1:T(8,128)(2,1)} %bitcast.24) | data formatting | bytes 2097152 | tf_op jit(solution)/shard_map/transpose | solution.py:384
  85.3 0.0 copy-start.2
  85.3 2.1 %gather.1 = bf16[8,4,16,16]{3,2,1,0:T(8,128)(2,1)} custom-call(s32[8]{0:T(128)} %bitcast.32, bf16[4,128,1024]{2,1,0:T(8,128)(2,1)} %bitcast.25), custom_call_target="tpu_custom_call" | custom-call | tf_op jit(solution)/shard_map/gather/pallas_call | solution.py:328
  87.4 1.1 %reshape.77 = bf16[16,512]{1,0:T(8,128)(2,1)S(1)} reshape(bf16[8,4,16,16]{3,2,1,0:T(8,128)(2,1)} %gather.1) | data formatting | bytes 32768 | tf_op jit(solution)/shard_map/reshape | solution.py:387
  88.5 0.0 copy-done.1
  88.5 0.4 fusion.20
  88.9 0.0 copy-done
  88.9 0.1 fusion.2
  89.0 0.0 copy-done.2
  89.0 0.1 broadcast_select_fusion
  89.1 0.6 pad.5.in_ref
  89.7 8.4 %swap.1 = f32[8,8,128]{2,1,0:T(8,128)} custom-call(f32[8,8,128]{2,1,0:T(8,128)} %pad.5.in_ref), custom_call_target="tpu_custom_call" | custom-call | tf_op jit(solution)/shard_map/swap/pallas_call | solution.py:364
  98.1 1.4 %slice_bitcast_fusion = f32[1,8,1,2,16]{4,3,2,1,0:T(2,128)} fusion(f32[8,8,128]{2,1,0:T(8,128)} %swap.1), kind=kLoop, calls=%fused_computation.7 | loop fusion | bytes 2048
  (5 shorter events, 0.0 us)
Async XLA Ops:
  0.6 88.2 %copy-start = (bf16[1024,16]{0,1:T(8,128)(2,1)S(1)}, bf16[1024,16]{0,1:T(8,128)(2,1)}, u32[]{:S(2)}) copy-start(bf16[1024,16]{0,1:T(8,128)(2,1)} %param.11) | copy-start | bytes 98308
  82.8 5.6 %copy-start.1 = (bf16[512,2048]{1,0:T(8,128)(2,1)S(1)}, bf16[512,2048]{1,0:T(8,128)(2,1)}, u32[]{:S(2)}) copy-start(bf16[512,2048]{1,0:T(8,128)(2,1)} %constant.49.clone) | copy-start | bytes 6291460
  85.3 3.7 %copy-start.2 = (s32[1,8]{1,0:T(1,128)S(1)}, s32[1,8]{1,0:T(1,128)}, u32[]{:S(2)}) copy-start(s32[1,8]{1,0:T(1,128)} %param.13) | copy-start | bytes 100

commit v3 on v2

--- a/solution.py
+++ b/solution.py
@@ -67,7 +67,7 @@
 
 def propagate_kernel(
     layers, strips, launch_ref, scr_ref, scrt_ref, g_ref, out_ref,
-    gall, gmat, srow, scol, sendbuf, recvbuf, slab, swapped, mid,
+    gall, gmat, early_row, early_col, stage_row, stage_col, srow, scol, sendbuf, recvbuf, slab, swapped, mid,
     gsend, grecv, ssend, srecv, xsend, xrecv, osend, orecv,
 ):
     count = layers * strips
@@ -99,27 +99,51 @@
     for k in range(1, layers):
         a = lax.rem(sec + k, layers)
         remote(g_ref, gall.at[sec], gsend, grecv.at[sec], a, strip).start()
-    for lay in range(layers):
-        if lay % 2 == 0:
-            @pl.when(sec == lay)
-            def _(lay=lay):
+    def to_all(start_one):
+        half = strips // 2
+
+        def far(i, _):
+            other = lax.rem(strip // half + 1, 2) * half + lax.rem(strip + i // layers, half)
+            start_one(lax.rem(sec + i, layers), other)
+            return 0
+
+        def near(i, _):
+            other = strip // half * half + lax.rem(strip + i // layers, half)
+            start_one(lax.rem(sec + i, layers), other)
+            return 0
+
+        lax.fori_loop(0, half * layers, far, 0)
+        lax.fori_loop(1, half * layers, near, 0)
+
+    rows_of = [(stage_row, early_row)] + [(scr_ref, srow.at[i]) for i in range(layers // 2 - 1)]
+    cols_of = [(stage_col, early_col)] + [(scrt_ref, scol.at[i]) for i in range(layers // 2 - 1)]
+
+    def share(lay):
+        @pl.when(sec == lay)
+        def _():
+            if lay % 2 == 0:
+                src, dst = rows_of[lay // 2]
+                if lay < 2:
+                    src[...] = scr_ref[...].astype(BF16)
                 for k in range(1, layers):
                     a = lax.rem(sec + k, layers)
-                    remote(scr_ref.at[a], srow.at[lay // 2], ssend, srecv.at[lay], a, strip).start()
-                srow[lay // 2] = scr_ref[lay]
-        else:
-            @pl.when(sec == lay)
-            def _(lay=lay):
-                def give(k, _):
-                    peer = lax.rem(me + k, count)
+                    remote(src.at[a], dst, ssend, srecv.at[lay], a, strip).start()
+                dst[...] = src[lay]
+            else:
+                src, dst = cols_of[lay // 2]
+                if lay < 2:
+                    src[...] = scrt_ref[...].astype(BF16)
+
+                def one(a, s):
                     remote(
-                        scrt_ref.at[peer], scol.at[lay // 2, strip], ssend, srecv.at[lay],
-                        lax.rem(peer, layers), peer // layers,
+                        src.at[s * layers + a], dst.at[strip], ssend, srecv.at[lay], a, s
                     ).start()
-                    return 0
-
-                lax.fori_loop(1, count, give, 0)
-                scol[lay // 2, strip] = scrt_ref[me]
+
+                to_all(one)
+                dst[strip] = src[me]
+
+    for lay in range(2):
+        share(lay)
     gall[sec] = g_ref[...]
 
     def build(lay):
@@ -141,23 +165,25 @@
 
     def screen_of(lay):
         if lay % 2 == 0:
+            src, dst = rows_of[lay // 2]
+
             @pl.when(sec != lay)
             def _():
-                remote(scr_ref.at[0], srow.at[lay // 2], ssend, srecv.at[lay], sec, strip).wait_recv()
-            return sincos(srow[lay // 2])
+                remote(src.at[0], dst, ssend, srecv.at[lay], sec, strip).wait_recv()
+            return sincos(dst[...].astype(F32))
+
+        dst = cols_of[lay // 2][1]
 
         @pl.when(sec != lay)
         def _():
-            whole = scol.at[lay // 2]
-            remote(whole, whole, ssend, srecv.at[lay], sec, strip).wait_recv()
+            remote(dst, dst, ssend, srecv.at[lay], sec, strip).wait_recv()
 
         @pl.when(sec == lay)
         def _():
-            most = scol.at[lay // 2, pl.ds(0, strips - 1)]
+            most = dst.at[pl.ds(0, strips - 1)]
             remote(most, most, ssend, srecv.at[lay], sec, strip).wait_recv()
 
-        theta = jnp.concatenate([scol[lay // 2, s] for s in range(strips)], axis=1)
-        return sincos(theta)
+        return sincos(jnp.concatenate([dst[s].astype(F32) for s in range(strips)], axis=1))
 
     def put(fc, value):
         rounded = value.astype(BF16)
@@ -190,15 +216,13 @@
 
         lax.fori_loop(0, length // block, body, 0)
 
-        def give(k, _):
-            peer = lax.rem(me + k, count)
+        def one(a, s):
             remote(
-                sendbuf.at[step, peer], recvbuf.at[step, me], xsend.at[step], xrecv.at[step],
-                lax.rem(peer, layers), peer // layers,
+                sendbuf.at[step, s * layers + a], recvbuf.at[step, me],
+                xsend.at[step], xrecv.at[step], a, s,
             ).start()
-            return 0
-
-        lax.fori_loop(1, count, give, 0)
+
+        to_all(one)
         recvbuf[step, me] = sendbuf[step, me]
 
     def arrived(step):
@@ -248,6 +272,9 @@
         build(lay)
     for lay in range(1, layers):
         arrived(lay - 1)
+        if lay == 1:
+            for late in range(2, layers):
+                share(late)
         along(lay - 1)
         screened(lay, lambda fc: mid[fc * lines:(fc + 1) * lines, :])
         across(lay, lay)
@@ -266,9 +293,9 @@
         @pl.when(sec == lay)
         def _(lay=lay):
             if lay % 2 == 0:
-                some = scr_ref.at[pl.ds(0, layers - 1)]
+                some = rows_of[lay // 2][0].at[pl.ds(0, layers - 1)]
             else:
-                some = scrt_ref.at[pl.ds(0, count - 1)]
+                some = cols_of[lay // 2][0].at[pl.ds(0, count - 1)]
             remote(some, some, ssend, srecv.at[lay], sec, strip).wait_send()
     for step in range(layers):
         most = sendbuf.at[step, pl.ds(0, count - 1)]
@@ -290,8 +317,12 @@
         scratch_shapes=[
             pltpu.VMEM((layers, 8, length), F32),
             pltpu.VMEM((layers, 2, length, length), BF16),
-            pltpu.VMEM((layers // 2, lines, length), F32),
-            pltpu.VMEM((layers // 2, strips, lines, rows), F32),
+            pltpu.VMEM((lines, length), BF16),
+            pltpu.VMEM((strips, lines, rows), BF16),
+            pltpu.VMEM((layers, lines, length), BF16),
+            pltpu.VMEM((count, lines, rows), BF16),
+            pltpu.VMEM((layers // 2 - 1, lines, length), F32),
+            pltpu.VMEM((layers // 2 - 1, strips, lines, rows), F32),
             pltpu.VMEM((layers, count, lines, 4 * lines), BF16),
             pltpu.VMEM((layers, count, lines, 4 * lines), BF16),
             pltpu.VMEM((4 * lines, length), BF16),

time: 99.9 us -> 102 us (1.021)
  Pallas kernels: 87.5 us -> 89.3 us
    pallas_call x1, Pallas kernels: 77 us -> 80 us  [propagate(): pl.pallas_call(functools.partial(propagate_kernel, layers, strips), out_s...]
    pallas_call x1, Pallas kernels: 8.4 us -> 7.21 us  [swap_strips(): pl.pallas_call(functools.partial(swap_kernel, strips), out_shape=jax.Shap...]
where the time goes in v3:
time: 102 us; the launch traced here: 101 us
  Pallas kernels  89.3 us (88%)
  local copies, waits for them, and re-layouts  8.2 us (8%)
  matrix products  1.99 us (2%)
  between operations  1.36 us (1%)
    pallas_call x1, Pallas kernels, propagate(): pl.pallas_call(functools.partial(propagate_kernel, layers, strips), out_s...  80 us
    pallas_call x1, Pallas kernels, swap_strips(): pl.pallas_call(functools.partial(swap_kernel, strips), out_shape=jax.Shap...  7.21 us
    transpose x1, local copies, waits for them, and re-layouts, per_device(): pupil = done.transpose(1, 0, 2, 3).reshape(fields, 2, rows, length)  2.44 us
    pallas_call x1, Pallas kernels, gather_blocks(): pl.pallas_call(functools.partial(gather_kernel, pupil.shape[-1] // SUB),...  2.09 us

profile of v3, /device:TPU:0, one launch (start us, length us, event | category | flops | bytes accessed | tf_op | source)
XLA Modules:
  0.0 101.2 jit_solution(11734701491969809405)
XLA Ops:
  0.6 0.0 copy-start
  1.3 0.1 fusion.16
  1.4 1.5 %fusion.14 = f32[4,1024]{1,0:T(4,128)S(1)} fusion(bf16[512,1024]{1,0:T(8,128)(2,1)} %constant.48.clone, bf16[2,512]{1,0:T(2,128)(2,1)S(1)} %get-tuple-element.10, bf16[2,512]{1,0:T(2,128)(2,1)S(1)} %get-tuple-element.11), kind=kOutput, calls=%fused_computation.26 | convolution fusion | flops 4202496 | bytes 1069056 | tf_op jit(solution)/shard_map/dot_general | solution.py:49
  2.9 0.1 fusion.18
  3.0 0.1 fusion.4
  3.1 0.6 concatenate.7.g_ref
  3.8 2.0 %copy.21 = f32[1024,128]{1,0:T(8,128)} copy(f32[1024,128]{0,1:T(8,128)} %bitcast.27) | data formatting | bytes 1048576 | tf_op jit(solution)/shard_map/transpose | solution.py:340
  5.8 80.0 %propagate.1 = bf16[4,4,32,1024]{3,2,1,0:T(8,128)(2,1)} custom-call(bf16[4,4,32,1024]{3,2,1,0:T(8,128)(2,1)} %bitcast.30, f32[4,32,1024]{2,1,0:T(8,128)} %bitcast.28, f32[32,32,128]{2,1,0:T(8,128)} %bitcast.29, f32[8,1024]{1,0:T(8,128)} %concatenate.7.g_ref), custom_call_target="tpu_custom_call" | custom-call | tf_op jit(solution)/shard_map/propagate/pallas_call | solution.py:312
  85.8 0.0 copy-start.1
  85.8 2.4 %copy.22 = bf16[4,4,32,1024]{3,2,1,0:T(8,128)(2,1)} copy(bf16[4,4,32,1024]{3,2,0,1:T(8,128)(2,1)} %bitcast.24) | data formatting | bytes 2097152 | tf_op jit(solution)/shard_map/transpose | solution.py:415
  88.2 0.0 copy-start.2
  88.2 2.1 %gather.1 = bf16[8,4,16,16]{3,2,1,0:T(8,128)(2,1)} custom-call(s32[8]{0:T(128)} %bitcast.32, bf16[4,128,1024]{2,1,0:T(8,128)(2,1)} %bitcast.25), custom_call_target="tpu_custom_call" | custom-call | tf_op jit(solution)/shard_map/gather/pallas_call | solution.py:359
  90.3 1.1 %reshape.77 = bf16[16,512]{1,0:T(8,128)(2,1)S(1)} reshape(bf16[8,4,16,16]{3,2,1,0:T(8,128)(2,1)} %gather.1) | data formatting | bytes 32768 | tf_op jit(solution)/shard_map/reshape | solution.py:418
  91.4 0.0 copy-done.1
  91.4 0.4 fusion.20
  91.8 0.0 copy-done
  91.8 0.1 fusion.2
  91.9 0.0 copy-done.2
  92.0 0.1 broadcast_select_fusion
  92.0 0.6 pad.5.in_ref
  92.7 7.2 %swap.1 = f32[8,8,128]{2,1,0:T(8,128)} custom-call(f32[8,8,128]{2,1,0:T(8,128)} %pad.5.in_ref), custom_call_target="tpu_custom_call" | custom-call | tf_op jit(solution)/shard_map/swap/pallas_call | solution.py:395
  99.9 1.4 %slice_bitcast_fusion = f32[1,8,1,2,16]{4,3,2,1,0:T(2,128)} fusion(f32[8,8,128]{2,1,0:T(8,128)} %swap.1), kind=kLoop, calls=%fused_computation.7 | loop fusion | bytes 2048
  (5 shorter events, 0.0 us)
Async XLA Ops:
  0.6 91.2 %copy-start = (bf16[1024,16]{0,1:T(8,128)(2,1)S(1)}, bf16[1024,16]{0,1:T(8,128)(2,1)}, u32[]{:S(2)}) copy-start(bf16[1024,16]{0,1:T(8,128)(2,1)} %param.11) | copy-start | bytes 98308
  85.8 5.6 %copy-start.1 = (bf16[512,2048]{1,0:T(8,128)(2,1)S(1)}, bf16[512,2048]{1,0:T(8,128)(2,1)}, u32[]{:S(2)}) copy-start(bf16[512,2048]{1,0:T(8,128)(2,1)} %constant.49.clone) | copy-start | bytes 6291460
  88.2 3.7 %copy-start.2 = (s32[1,8]{1,0:T(1,128)S(1)}, s32[1,8]{1,0:T(1,128)}, u32[]{:S(2)}) copy-start(s32[1,8]{1,0:T(1,128)} %param.13) | copy-start | bytes 100

commit v4 on v3

--- a/solution.py
+++ b/solution.py
@@ -100,20 +100,12 @@
         a = lax.rem(sec + k, layers)
         remote(g_ref, gall.at[sec], gsend, grecv.at[sec], a, strip).start()
     def to_all(start_one):
-        half = strips // 2
-
-        def far(i, _):
-            other = lax.rem(strip // half + 1, 2) * half + lax.rem(strip + i // layers, half)
-            start_one(lax.rem(sec + i, layers), other)
+        def one(k, _):
+            peer = lax.rem(me + k, count)
+            start_one(lax.rem(peer, layers), peer // layers)
             return 0
 
-        def near(i, _):
-            other = strip // half * half + lax.rem(strip + i // layers, half)
-            start_one(lax.rem(sec + i, layers), other)
-            return 0
-
-        lax.fori_loop(0, half * layers, far, 0)
-        lax.fori_loop(1, half * layers, near, 0)
+        lax.fori_loop(1, count, one, 0)
 
     rows_of = [(stage_row, early_row)] + [(scr_ref, srow.at[i]) for i in range(layers // 2 - 1)]
     cols_of = [(stage_col, early_col)] + [(scrt_ref, scol.at[i]) for i in range(layers // 2 - 1)]
@@ -142,7 +134,7 @@
                 to_all(one)
                 dst[strip] = src[me]
 
-    for lay in range(2):
+    for lay in range(layers):
         share(lay)
     gall[sec] = g_ref[...]
 
@@ -202,7 +194,10 @@
     block = 256
 
     def across(lay, step):
-        def body(b, _):
+        per = block // lines
+
+        def body(i, _):
+            b = lax.rem(me // per + 1 + i, length // block)
             at = pl.ds(pl.multiple_of(b * block, block), block)
             dims = (((1,), (1,)), ((), ()))
             total = lax.dot_general(
@@ -210,19 +205,24 @@
             ) + lax.dot_general(
                 gmat[lay, 1, at, :], swapped[...], dims, preferred_element_type=F32
             )
-            per = block // lines
             sendbuf[step, pl.ds(b * per, per)] = total.reshape(per, lines, wide).astype(BF16)
+
+            def one(j, _):
+                peer = b * per + lax.rem(me + j, per)
+
+                @pl.when(peer != me)
+                def _():
+                    remote(
+                        sendbuf.at[step, peer], recvbuf.at[step, me], xsend.at[step],
+                        xrecv.at[step], lax.rem(peer, layers), peer // layers,
+                    ).start()
+                return 0
+
+            lax.fori_loop(0, per, one, 0)
             return 0
 
         lax.fori_loop(0, length // block, body, 0)
 
-        def one(a, s):
-            remote(
-                sendbuf.at[step, s * layers + a], recvbuf.at[step, me],
-                xsend.at[step], xrecv.at[step], a, s,
-            ).start()
-
-        to_all(one)
         recvbuf[step, me] = sendbuf[step, me]
 
     def arrived(step):
@@ -272,9 +272,6 @@
         build(lay)
     for lay in range(1, layers):
         arrived(lay - 1)
-        if lay == 1:
-            for late in range(2, layers):
-                share(late)
         along(lay - 1)
         screened(lay, lambda fc: mid[fc * lines:(fc + 1) * lines, :])
         across(lay, lay)

time: 102 us -> 93.4 us (0.916)
  Pallas kernels: 89.3 us -> 80.9 us
    pallas_call x1, Pallas kernels: 80 us -> 72.1 us  [propagate(): pl.pallas_call(functools.partial(propagate_kernel, layers, strips), out_s...]
where the time goes in v4:
time: 93.4 us; the launch traced here: 92.9 us
  Pallas kernels  80.9 us (87%)
  local copies, waits for them, and re-layouts  8.2 us (9%)
  matrix products  1.99 us (2%)
  between operations  1.36 us (1%)
    pallas_call x1, Pallas kernels, propagate(): pl.pallas_call(functools.partial(propagate_kernel, layers, strips), out_s...  72.1 us
    pallas_call x1, Pallas kernels, swap_strips(): pl.pallas_call(functools.partial(swap_kernel, strips), out_shape=jax.Shap...  6.79 us
    transpose x1, local copies, waits for them, and re-layouts, per_device(): pupil = done.transpose(1, 0, 2, 3).reshape(fields, 2, rows, length)  2.44 us
    pallas_call x1, Pallas kernels, gather_blocks(): pl.pallas_call(functools.partial(gather_kernel, pupil.shape[-1] // SUB),...  2.09 us
    transpose x1, local copies, waits for them, and re-layouts, propagate(): screen.T.reshape(count, lines, rows)  2.03 us

profile of v4, /device:TPU:0, one launch (start us, length us, event | category | flops | bytes accessed | tf_op | source)
XLA Modules:
  0.0 92.9 jit_solution(404228109470664228)
XLA Ops:
  0.6 0.0 copy-start
  1.3 0.1 fusion.16
  1.4 1.5 %fusion.14 = f32[4,1024]{1,0:T(4,128)S(1)} fusion(bf16[512,1024]{1,0:T(8,128)(2,1)} %constant.48.clone, bf16[2,512]{1,0:T(2,128)(2,1)S(1)} %get-tuple-element.10, bf16[2,512]{1,0:T(2,128)(2,1)S(1)} %get-tuple-element.11), kind=kOutput, calls=%fused_computation.26 | convolution fusion | flops 4202496 | bytes 1069056 | tf_op jit(solution)/shard_map/dot_general | solution.py:49
  2.9 0.1 fusion.18
  3.0 0.1 fusion.4
  3.1 0.6 concatenate.7.g_ref
  3.8 2.0 %copy.21 = f32[1024,128]{1,0:T(8,128)} copy(f32[1024,128]{0,1:T(8,128)} %bitcast.27) | data formatting | bytes 1048576 | tf_op jit(solution)/shard_map/transpose | solution.py:337
  5.8 72.1 %propagate.1 = bf16[4,4,32,1024]{3,2,1,0:T(8,128)(2,1)} custom-call(bf16[4,4,32,1024]{3,2,1,0:T(8,128)(2,1)} %bitcast.30, f32[4,32,1024]{2,1,0:T(8,128)} %bitcast.28, f32[32,32,128]{2,1,0:T(8,128)} %bitcast.29, f32[8,1024]{1,0:T(8,128)} %concatenate.7.g_ref), custom_call_target="tpu_custom_call" | custom-call | tf_op jit(solution)/shard_map/propagate/pallas_call | solution.py:309
  77.9 0.0 copy-start.1
  77.9 2.4 %copy.22 = bf16[4,4,32,1024]{3,2,1,0:T(8,128)(2,1)} copy(bf16[4,4,32,1024]{3,2,0,1:T(8,128)(2,1)} %bitcast.24) | data formatting | bytes 2097152 | tf_op jit(solution)/shard_map/transpose | solution.py:412
  80.3 0.0 copy-start.2
  80.3 2.1 %gather.1 = bf16[8,4,16,16]{3,2,1,0:T(8,128)(2,1)} custom-call(s32[8]{0:T(128)} %bitcast.32, bf16[4,128,1024]{2,1,0:T(8,128)(2,1)} %bitcast.25), custom_call_target="tpu_custom_call" | custom-call | tf_op jit(solution)/shard_map/gather/pallas_call | solution.py:356
  82.4 1.1 %reshape.77 = bf16[16,512]{1,0:T(8,128)(2,1)S(1)} reshape(bf16[8,4,16,16]{3,2,1,0:T(8,128)(2,1)} %gather.1) | data formatting | bytes 32768 | tf_op jit(solution)/shard_map/reshape | solution.py:415
  83.5 0.0 copy-done.1
  83.5 0.4 fusion.20
  83.9 0.0 copy-done
  83.9 0.1 fusion.2
  84.0 0.0 copy-done.2
  84.0 0.1 broadcast_select_fusion
  84.1 0.6 pad.5.in_ref
  84.7 6.8 %swap.1 = f32[8,8,128]{2,1,0:T(8,128)} custom-call(f32[8,8,128]{2,1,0:T(8,128)} %pad.5.in_ref), custom_call_target="tpu_custom_call" | custom-call | tf_op jit(solution)/shard_map/swap/pallas_call | solution.py:392
  91.5 1.4 %slice_bitcast_fusion = f32[1,8,1,2,16]{4,3,2,1,0:T(2,128)} fusion(f32[8,8,128]{2,1,0:T(8,128)} %swap.1), kind=kLoop, calls=%fused_computation.7 | loop fusion | bytes 2048
  (5 shorter events, 0.0 us)
Async XLA Ops:
  0.6 83.3 %copy-start = (bf16[1024,16]{0,1:T(8,128)(2,1)S(1)}, bf16[1024,16]{0,1:T(8,128)(2,1)}, u32[]{:S(2)}) copy-start(bf16[1024,16]{0,1:T(8,128)(2,1)} %param.11) | copy-start | bytes 98308
  77.9 5.6 %copy-start.1 = (bf16[512,2048]{1,0:T(8,128)(2,1)S(1)}, bf16[512,2048]{1,0:T(8,128)(2,1)}, u32[]{:S(2)}) copy-start(bf16[512,2048]{1,0:T(8,128)(2,1)} %constant.49.clone) | copy-start | bytes 6291460
  80.3 3.7 %copy-start.2 = (s32[1,8]{1,0:T(1,128)S(1)}, s32[1,8]{1,0:T(1,128)}, u32[]{:S(2)}) copy-start(s32[1,8]{1,0:T(1,128)} %param.13) | copy-start | bytes 100
